TPU v7x, 32 devices: a whole 2x2x4 slice. The times are simulated.
32 devices in a mesh: group: 4 (over z), blk: 8 (over y, x, core).
Axes of the slice: x: 2, y: 2, z: 4, core: 2. Of those that a mesh axis runs over, the one named last changes fastest.
Arguments:
- cotangent: bfloat16 [24576, 3584], P(('group', 'blk')), may hold values from -6 to 6
- pre_act: bfloat16 [24576, 2, 1024], P(('group', 'blk')), may hold values from -6 to 6
- down_weight: bfloat16 [1024, 2, 3584], P('blk'), may hold values from -0.09375 to 0.09375
- tile_expert: int32 [192], P(('group', 'blk')), may hold values from 0 to 1
- tile_fill: int32 [192], P(('group', 'blk')), may hold values from 1 to 128, as said below
Outputs:
- act_grad: bfloat16 [24576, 2, 1024], P(('group', 'blk'))
- weight_grad: float32 [1024, 2, 3584], P(('group', 'blk'))
Inputs may be any that keep to these rules, and one draw needn't show every extreme that they name: tile_fill reaches 128 in every draw.
All inputs are finite; a program needn't handle non-finite values.
Results may differ from a plain program's by a relative error of at most 0.0029.
Values may be sent and summed in bfloat16 or wider, within the bound.
No kernel may reach another device: no remote copies, remote signals or barrier semaphores. Data moves between devices by JAX's collectives and lax.ppermute only.
A program may use at most 192 MiB of HBM per device.

v0:
```python
import jax
import jax.numpy as jnp
from jax import lax
from jax.sharding import PartitionSpec as P

grad_factor = 0.015625


def body(cotangent, pre_act, down_weight, tile_expert, tile_fill):
    row_count = cotangent.shape[0]
    tile_count = tile_expert.shape[0]
    tile_size = row_count // tile_count
    width = cotangent.shape[1]
    hidden_units = pre_act.shape[2]
    expert_count = down_weight.shape[1]
    cot_tiles = cotangent.reshape(tile_count, tile_size, width)
    piece = lax.all_gather(down_weight, "blk", axis=0, tiled=True)
    chosen = jnp.take(piece, tile_expert, axis=1)
    result = jnp.einsum("trd,ntd->trn", cot_tiles, chosen, preferred_element_type=jnp.float32)
    hidden_grad = result.reshape(row_count, piece.shape[0])
    positions = jnp.arange(tile_size, dtype=jnp.int32)
    live_rows = (positions[None, :] < tile_fill[:, None]).astype(jnp.float32).reshape(row_count, 1)
    gate_pre = pre_act[:, 0, :].astype(jnp.float32)
    up_pre = pre_act[:, 1, :].astype(jnp.float32)
    sigmoid_gate = jax.nn.sigmoid(gate_pre)
    silu_gate = gate_pre * sigmoid_gate
    activation = (live_rows * silu_gate * up_pre).astype(jnp.bfloat16)
    gate_grad = (
        live_rows * hidden_grad * up_pre * sigmoid_gate * (1.0 + gate_pre * (1.0 - sigmoid_gate))
    )
    up_grad = live_rows * hidden_grad * silu_gate
    act_grad = jnp.stack([gate_grad, up_grad], axis=1).astype(jnp.bfloat16)
    expert_hot = tile_expert[:, None] == jnp.arange(expert_count, dtype=jnp.int32)[None, :]
    group_count = lax.axis_size("group")
    blk_count = lax.axis_size("blk")
    block_rows = hidden_units // (group_count * blk_count)
    reordered = activation.reshape(row_count, group_count, blk_count, block_rows)
    reordered = jnp.swapaxes(reordered, 1, 2).reshape(tile_count, tile_size, 1, hidden_units)
    act_expert = jnp.where(expert_hot[:, None, :, None], reordered, jnp.zeros((), jnp.bfloat16))
    partial_value = lax.psum_scatter(
        jnp.einsum("treh,trd->hed", act_expert, cot_tiles, preferred_element_type=jnp.float32),
        "blk",
        scatter_dimension=0,
        tiled=True,
    )
    total = lax.psum_scatter(partial_value, "group", scatter_dimension=0, tiled=True)
    return (act_grad, total * grad_factor)


def solution(mesh):
    placed = (
        P(("group", "blk"), None),
        P(("group", "blk"), None, None),
        P("blk", None, None),
        P(("group", "blk")),
        P(("group", "blk")),
    )
    return jax.shard_map(
        body,
        mesh=mesh,
        in_specs=placed,
        out_specs=(P(("group", "blk"), None, None), P(("group", "blk"), None, None)),
        check_vma=False,
    )
```

profile of v0, /device:TPU:0, one launch (start us, length us, event | category | flops | bytes accessed | tf_op | source)
XLA Modules:
  0.0 364.5 jit_solution(18192206110724580482)
XLA Ops:
  7.2 0.0 all-gather.2.cloned.1.call-start
  7.2 5.7 %copy.10 = bf16[128,2,3584]{0,2,1:T(8,128)(2,1)} copy(bf16[128,2,3584]{2,1,0:T(2,128)(2,1)} %param.7) | data formatting | bytes 3670016 | tf_op args[2]
  12.9 0.0 all-gather.2.cloned.1.call-update
  12.9 0.0 reduce-scatter.3.cloned.1.call-start
  13.0 5.8 %fusion.18 = (bf16[768,1,1024]{2,1,0:T(2,128)(2,1)}, bf16[768,1,1024]{2,1,0:T(2,128)(2,1)}) fusion(bf16[768,2,1024]{2,1,0:T(2,128)(2,1)S(1)} %copy-done.4), kind=kLoop, calls=%fused_computation.36 | loop fusion | bytes 6291456 | tf_op jit(solution)/shard_map/slice | solution.py:24
  18.8 6.8 %copy.21 = bf16[768,1,1024]{0,2,1:T(8,128)(2,1)S(1)} copy(bf16[768,1,1024]{2,1,0:T(2,128)(2,1)} %get-tuple-element.12) | data formatting | bytes 3145728
  25.7 7.1 %copy.22 = bf16[768,1,1024]{0,2,1:T(8,128)(2,1)S(1)} copy(bf16[768,1,1024]{2,1,0:T(2,128)(2,1)} %get-tuple-element.13) | data formatting | bytes 3145728
  32.8 0.1 convert_bitcast_fusion
  32.9 0.7 copy-done.5
  33.6 1.2 fusion.13
  34.8 1.3 copy.15
  36.1 4.3 %broadcast_in_dim.43 = bf16[6,128,1024]{1,0,2:T(8,128)(2,1)} reshape(bf16[768,8,4,32]{0,3,2,1:T(8,128)(2,1)} %copy.15) | data formatting | bytes 3145728 | tf_op jit(solution)/shard_map/jit(_where)/broadcast_in_dim | solution.py:39
  40.4 1.8 copy.16
  42.2 19.2 %convolution_bitcast_fusion = f32[1024,2,3584]{2,0,1:T(8,128)} fusion(bf16[6,128,3584,1]{2,1,0,3:T(8,128)(2,1)} %bitcast.36, pred[6,2]{0,1:T(4,128)(4,1)S(1)} %iota_compare_fusion.1, bf16[6,128,1024]{1,2,0:T(8,128)(2,1)S(1)} %copy.16), kind=kOutput, calls=%fused_computation.14 | convolution fusion | flops 11275862016 | bytes 36438028 | tf_op jit(solution)/shard_map/treh,trd->hed/dot_general | solution.py:41
  61.4 0.0 reduce-scatter.3.cloned.1.call-update
  61.5 0.2 reduce-scatter.5.cloned.1.call-start
  61.7 37.8 %all-gather.2.cloned.1.call-done = bf16[1024,2,3584]{0,2,1:T(8,128)(2,1)} async-done(((bf16[128,2,3584]{0,2,1:T(8,128)(2,1)}), bf16[1024,2,3584]{0,2,1:T(8,128)(2,1)}) %all-gather.2.cloned.1.call-update) | async-done | bytes 14680080 | tf_op jit(solution)/shard_map/all_gather | solution.py:17
  99.6 11.3 %fusion.17 = (bf16[1024,2,896]{0,2,1:T(8,128)(2,1)}, bf16[1024,2,896]{0,2,1:T(8,128)(2,1)}, bf16[1024,2,896]{0,2,1:T(8,128)(2,1)}, bf16[1024,2,896]{0,2,1:T(8,128)(2,1)}) fusion(bf16[1024,2,3584]{0,2,1:T(8,128)(2,1)} %all-gather.2.cloned.1.call-done), kind=kLoop, calls=%fused_computation.35 | loop fusion | bytes 29360128 | tf_op jit(solution)/shard_map/jit(_take)/gather | solution.py:18
  110.9 10.1 %gather_fusion = bf16[6,1024,896]{1,2,0:T(8,128)(2,1)} fusion(bf16[1024,2,896]{0,2,1:T(8,128)(2,1)} %get-tuple-element.6, s32[1024]{0:T(1024)S(1)} %pad_clamp_fusion), kind=kCustom, calls=%fused_computation | custom fusion | bytes 22020120 | tf_op jit(solution)/shard_map/jit(_take)/gather | solution.py:18
  120.9 10.3 %gather_fusion.1 = bf16[6,1024,896]{1,2,0:T(8,128)(2,1)} fusion(bf16[1024,2,896]{0,2,1:T(8,128)(2,1)} %get-tuple-element.8, s32[1024]{0:T(1024)S(1)} %pad_clamp_fusion), kind=kCustom, calls=%fused_computation.1 | custom fusion | bytes 22020120 | tf_op jit(solution)/shard_map/jit(_take)/gather | solution.py:18
  131.3 10.3 %gather_fusion.2 = bf16[6,1024,896]{1,2,0:T(8,128)(2,1)} fusion(bf16[1024,2,896]{0,2,1:T(8,128)(2,1)} %get-tuple-element.7, s32[1024]{0:T(1024)S(1)} %pad_clamp_fusion), kind=kCustom, calls=%fused_computation.2 | custom fusion | bytes 22020120 | tf_op jit(solution)/shard_map/jit(_take)/gather | solution.py:18
  141.6 7.9 %gather_fusion.3 = bf16[6,1024,896]{1,2,0:T(8,128)(2,1)} fusion(bf16[1024,2,896]{0,2,1:T(8,128)(2,1)} %get-tuple-element.9, s32[1024]{0:T(1024)S(1)} %pad_clamp_fusion), kind=kCustom, calls=%fused_computation.3 | custom fusion | bytes 22020120 | tf_op jit(solution)/shard_map/jit(_take)/gather | solution.py:18
  149.5 134.7 %reduce-scatter.3.cloned.1.call-done = f32[128,2,3584]{2,0,1:T(8,128)} async-done(((f32[1024,2,3584]{2,0,1:T(8,128)}), f32[128,2,3584]{2,0,1:T(8,128)}) %reduce-scatter.3.cloned.1.call-update) | async-done | bytes 3670032 | tf_op jit(solution)/shard_map/reduce_scatter | solution.py:40
  284.2 0.0 reduce-scatter.5.cloned.1.call-update
  284.2 20.2 %fusion = f32[6,1024,128]{1,2,0:T(8,128)} fusion(bf16[6,128,3584]{2,1,0:T(8,128)(2,1)} %bitcast.37, bf16[1024,6,896]{0,2,1:T(8,128)(2,1)} %bitcast.32, bf16[1024,6,896]{0,2,1:T(8,128)(2,1)} %bitcast.31, bf16[1024,6,896]{0,2,1:T(8,128)(2,1)} %bitcast.30, bf16[1024,6,896]{0,2,1:T(8,128)(2,1)} %bitcast.29, pred[6]{0:T(512)(128)(4,1)S(1)} %compare_and_fusion), kind=kOutput, calls=%fused_computation.5 | convolution fusion | flops 5835325440 | bytes 52690952 | tf_op jit(solution)/shard_map/trd,ntd->trn/dot_general | solution.py:19
  304.4 3.7 %copy.12 = f32[768,1,1024]{0,2,1:T(8,128)} copy(f32[768,1,1024]{2,0,1:T(8,128)} %bitcast.35) | data formatting | bytes 6291456 | tf_op jit(solution)/shard_map/reshape | solution.py:20
  308.1 3.5 multiply_convert_fusion.2
  311.6 0.3 pad_maximum_fusion
  311.9 5.8 %copy.17 = bf16[768,2,1024]{2,1,0:T(2,128)(2,1)} copy(bf16[768,2,1024]{0,2,1:T(8,128)(2,1)S(1)} %pad_maximum_fusion) | data formatting | bytes 6291456
  317.7 37.4 %reduce-scatter.5.cloned.1.call-done = f32[32,2,3584]{2,0,1:T(8,128)} async-done(((f32[128,2,3584]{2,0,1:T(8,128)}), f32[32,2,3584]{2,0,1:T(8,128)}) %reduce-scatter.5.cloned.1.call-update) | async-done | bytes 917520 | tf_op jit(solution)/shard_map/reduce_scatter | solution.py:46
  355.1 1.2 broadcast_multiply_fusion
  356.4 1.6 copy.18
  (21 shorter events, 0.1 us)
Async XLA Ops:
  7.2 5.8 %copy-start.4 = (bf16[768,2,1024]{2,1,0:T(2,128)(2,1)S(1)}, bf16[768,2,1024]{2,1,0:T(2,128)(2,1)}, u32[]{:S(2)}) copy-start(bf16[768,2,1024]{2,1,0:T(2,128)(2,1)} %param.6) | copy-start | bytes 9437188
  7.2 92.4 %all-gather.2.cloned.1.call-start = ((), (), s32[]{:S(2)}) async-start(), calls=%async_computation.2 | async-start | bytes 16515072 | tf_op jit(solution)/shard_map/all_gather | solution.py:17
  12.9 271.3 %reduce-scatter.3.cloned.1.call-start = ((), (), s32[]{:S(2)}) async-start(), calls=%async_computation.3 | async-start | bytes 33030144 | tf_op jit(solution)/shard_map/reduce_scatter | solution.py:40
  25.6 9.1 %copy-start = (bf16[768,1,1024]{0,2,1:T(8,128)(2,1)}, bf16[768,1,1024]{0,2,1:T(8,128)(2,1)S(1)}, u32[]{:S(2)}) copy-start(bf16[768,1,1024]{0,2,1:T(8,128)(2,1)S(1)} %copy.21) | copy-start | bytes 4718596
  25.6 7.1 %copy-start.7 = (s32[6]{0:T(128)S(1)}, s32[6]{0:T(128)}, u32[]{:S(2)}) copy-start(s32[6]{0:T(128)} %param.9) | copy-start | bytes 76
  32.8 3.3 copy-start.2
  32.9 0.7 copy-start.5
  36.1 6.1 %copy-start.8 = (s32[6]{0:T(128)S(1)}, s32[6]{0:T(128)}, u32[]{:S(2)}) copy-start(s32[6]{0:T(128)} %param.8) | copy-start | bytes 76
  61.5 293.7 %reduce-scatter.5.cloned.1.call-start = ((), (), s32[]{:S(2)}) async-start(), calls=%async_computation.4 | async-start | bytes 4587520 | tf_op jit(solution)/shard_map/reduce_scatter | solution.py:46
  304.4 3.7 %copy-start.1 = (bf16[768,1,1024]{0,2,1:T(8,128)(2,1)S(1)}, bf16[768,1,1024]{0,2,1:T(8,128)(2,1)}, u32[]{:S(2)}) copy-start(bf16[768,1,1024]{0,2,1:T(8,128)(2,1)} %copy-done) | copy-start | bytes 4718596
  304.4 3.7 %copy-start.3 = (bf16[768,1,1024]{0,2,1:T(8,128)(2,1)S(1)}, bf16[768,1,1024]{0,2,1:T(8,128)(2,1)}, u32[]{:S(2)}) copy-start(bf16[768,1,1024]{0,2,1:T(8,128)(2,1)} %copy-done.2) | copy-start | bytes 4718596
  304.4 3.7 %copy-start.6 = (f32[768]{0:T(1024)S(1)}, f32[768]{0:T(1024)}, u32[]{:S(2)}) copy-start(f32[768]{0:T(1024)} %copy-done.5) | copy-start | bytes 9220
Sparse Core Ops, SparseCore 0:
  13.0 86.4 all-gather.1
  103.2 180.9 reduce-scatter.2
  286.5 68.5 reduce-scatter.4
where the time goes:
time: 365 us
  waiting for transfers between devices  210 us (58%)
  local copies, waits for them, and re-layouts  94.6 us (26%)
  matrix products  39.4 us (11%)
  between operations  13.9 us (4%)
  other arithmetic  6.35 us (2%)
    reduce_scatter x1, waiting for transfers between devices, body(): lax.psum_scatter(jnp.einsum('treh,trd->hed', act_expert, cot_tiles, prefe...  135 us
    gather x5, local copies, waits for them, and re-layouts, body(): chosen = jnp.take(piece, tile_expert, axis=1)  49.9 us
    all_gather x1, waiting for transfers between devices, body(): piece = lax.all_gather(down_weight, 'blk', axis=0, tiled=True)  37.8 us
    reduce_scatter x1, waiting for transfers between devices, body(): lax.psum_scatter(partial_value, 'group', scatter_dimension=0, tiled=True)  37.4 us
    unnamed x23, local copies, waits for them, and re-layouts  27.7 us
    dot_general x1, matrix products, body(): jnp.einsum('trd,ntd->trn', cot_tiles, chosen, preferred_element_type=jnp....  20.2 us
    dot_general x1, matrix products, body(): jnp.einsum('treh,trd->hed', act_expert, cot_tiles, preferred_element_type...  19.2 us
  transfers between devices with their start and end apart: 3, of which 3 were waited for; matrix products, arithmetic and copies ran while one was open for 36% of the time, Pallas kernels for 0%

commit v1 on v0

v1 whole, which is shorter than its diff:
```python
import functools

import jax
import jax.numpy as jnp
from jax import lax
from jax.experimental import pallas as pl
from jax.experimental.pallas import tpu as pltpu
from jax.sharding import PartitionSpec as P


grad_factor = 0.015625
MIB = 1024 * 1024


def bits_of(size):
    return [1 << i for i in range(size.bit_length() - 1)]


def flip(value, axis, size, mask):
    return lax.ppermute(value, axis, [(i, i ^ mask) for i in range(size)])


def params(mib):
    return pltpu.CompilerParams(vmem_limit_bytes=mib * MIB)


def cost(flops, size):
    return pl.CostEstimate(flops=flops, bytes_accessed=size, transcendentals=0)


def gate_terms(pre_ref, fill):
    pre = jnp.swapaxes(pre_ref[...], 0, 1)
    gate, up = pre[0].astype(jnp.float32), pre[1].astype(jnp.float32)
    position = lax.broadcasted_iota(jnp.int32, (gate.shape[0], 1), 0)
    live = (position < fill).astype(jnp.float32)
    sig = 1.0 / (1.0 + jnp.exp(-gate))
    return live, gate, up, sig


def activation_kernel(fill_ref, pre_ref, out_ref):
    live, gate, up, sig = gate_terms(pre_ref, fill_ref[pl.program_id(0)])
    out_ref[...] = (live * (gate * sig) * up).T.astype(out_ref.dtype)


def activation_t(tile_fill, pre_act):
    tiles = tile_fill.shape[0]
    rows, two, hidden = pre_act.shape
    tile = rows // tiles
    return pl.pallas_call(
        activation_kernel,
        grid_spec=pltpu.PrefetchScalarGridSpec(
            num_scalar_prefetch=1,
            grid=(tiles,),
            in_specs=[pl.BlockSpec((tile, two, hidden), lambda t, f: (t, 0, 0))],
            out_specs=pl.BlockSpec((hidden, tile), lambda t, f: (0, t)),
        ),
        out_shape=jax.ShapeDtypeStruct((hidden, rows), pre_act.dtype),
        compiler_params=params(58),
        cost_estimate=cost(0, 6 * rows * hidden),
        name="activation_t",
    )(tile_fill, pre_act)


def part_rows(core_ref, mine, rows, granules, move):
    def blocks(granule):
        for j in range(rows // (2 * granule)):
            keep = pl.multiple_of((2 * j + mine) * granule, granule)
            send = pl.multiple_of((2 * j + 1 - mine) * granule, granule)
            move(pl.ds(j * granule, granule), pl.ds(keep, granule), pl.ds(send, granule))

    if granules[0] == granules[1]:
        blocks(granules[0])
    else:
        for core in range(2):
            pl.when(core_ref == core)(functools.partial(blocks, granules[core]))


def term_kernel(granules, first, count, tiles, ids_ref, pos_ref, own_ref, other_ref, cot_ref, cot2_ref, send, keep, acc):
    tile = own_ref.shape[1] // tiles

    def masked(act_ref, start, e):
        parts = []
        for t in range(tiles):
            part = act_ref[:, t * tile : (t + 1) * tile]
            parts.append(jnp.where(ids_ref[start + t] == e, part, jnp.zeros_like(part)))
        return jnp.concatenate(parts, axis=1)

    for e in range(send.shape[0]):
        acc[...] = jnp.dot(
            masked(own_ref, 0, e), cot_ref[:, first : first + count], preferred_element_type=jnp.float32
        ) + jnp.dot(
            masked(other_ref, tiles, e), cot2_ref[:, first : first + count], preferred_element_type=jnp.float32
        )

        def move(to, kept, sent):
            keep[e, to, :] = acc[kept, :]
            send[e, to, :] = acc[sent, :].astype(send.dtype)

        part_rows(pos_ref[0], pos_ref[1], acc.shape[0], granules, move)


def terms(ids, pos, own_t, other_t, cot, cot2, granules, experts, first, count, block):
    hidden, rows = own_t.shape
    half = cot.shape[1] // 2
    tiles = ids.shape[0] // 2
    return pl.pallas_call(
        functools.partial(term_kernel, granules, first, count, tiles),
        grid_spec=pltpu.PrefetchScalarGridSpec(
            num_scalar_prefetch=2,
            grid=(hidden // block,),
            in_specs=[
                pl.BlockSpec((block, rows), lambda g, i, p: (g, 0)),
                pl.BlockSpec((block, rows), lambda g, i, p: (g, 0)),
                pl.BlockSpec((rows, half), lambda g, i, p: (0, p[0])),
                pl.BlockSpec((rows, half), lambda g, i, p: (0, p[0])),
            ],
            out_specs=[pl.BlockSpec((experts, block // 2, count), lambda g, i, p: (0, g, 0))] * 2,
            scratch_shapes=[pltpu.VMEM((block, count), jnp.float32)],
        ),
        out_shape=[
            jax.ShapeDtypeStruct((experts, hidden // 2, count), jnp.bfloat16),
            jax.ShapeDtypeStruct((experts, hidden // 2, count), jnp.float32),
        ],
        compiler_params=params(58),
        cost_estimate=cost(4 * hidden * 2 * rows * count, 12 * hidden * count + 8 * rows * half),
        name="terms",
    )(ids, pos, own_t, other_t, cot, cot2)


def step_kernel(granules, step, pos_ref, keep_ref, recv_ref, *refs):
    send, keep, acc = refs[-3:]
    for e in range(keep_ref.shape[0]):
        acc[...] = keep_ref[e] + recv_ref[e].astype(jnp.float32)

        def move(to, kept, sent):
            keep[e, to, :] = acc[kept, :]
            send[e, to, :] = acc[sent, :].astype(send.dtype)

        part_rows(pos_ref[0], pos_ref[step], acc.shape[0], granules, move)


def halve(pos, step, keep, recv, granules, kind, after=()):
    experts, rows, count = keep.shape
    return pl.pallas_call(
        functools.partial(step_kernel, granules, step),
        in_specs=[pl.BlockSpec(memory_space=pltpu.SMEM)]
        + [pl.BlockSpec(memory_space=pltpu.VMEM)] * 2
        + [pl.BlockSpec(memory_space=pl.ANY)] * len(after),
        out_specs=[pl.BlockSpec(memory_space=pltpu.VMEM)] * 2,
        scratch_shapes=[pltpu.VMEM((rows, count), jnp.float32)],
        out_shape=[
            jax.ShapeDtypeStruct((experts, rows // 2, count), kind),
            jax.ShapeDtypeStruct((experts, rows // 2, count), jnp.float32),
        ],
        compiler_params=params(16),
        cost_estimate=cost(0, 9 * experts * rows * count),
        name="halve",
    )(pos, keep, recv, *after)


def finish_kernel(firsts, core_ref, *refs):
    out = refs[-1]
    keeps, others = refs[: len(firsts)], refs[len(firsts) : -1]
    half = out.shape[2] // 2
    for core in range(2):

        @pl.when(core_ref[0] == core)
        def _():
            for first, keep, other in zip(firsts, keeps, others):
                count = keep.shape[2]
                for e in range(out.shape[1]):
                    start = core * half + first
                    out[:, e, start : start + count] = keep[e] * grad_factor
                    start = (1 - core) * half + first
                    out[:, e, start : start + count] = other[e] * grad_factor


def finish(core, firsts, keeps, others, shape):
    return pl.pallas_call(
        functools.partial(finish_kernel, firsts),
        in_specs=[pl.BlockSpec(memory_space=pltpu.SMEM)] + [pl.BlockSpec(memory_space=pltpu.VMEM)] * (2 * len(firsts)),
        out_specs=pl.BlockSpec(memory_space=pltpu.VMEM),
        out_shape=jax.ShapeDtypeStruct(shape, jnp.float32),
        compiler_params=params(16),
        name="finish",
    )(core, *keeps, *others)


def grad_kernel(units, ids_ref, fill_ref, col_ref, slot_ref, cot_ref, pre_ref, *refs):
    parts = refs[: 2 * units]
    out_ref, raw, weight, grad, sems = refs[-5:]
    s, j = pl.program_id(0), pl.program_id(1)
    rows = parts[0].shape[0]
    wide = 2 * rows
    tile = cot_ref.shape[0] // 2

    def copy(i):
        to = pl.ds(pl.multiple_of(slot_ref[i] * rows, rows), rows)
        return pltpu.make_async_copy(parts[i], raw.at[i // 2, to], sems.at[i])

    @pl.when((s == 0) & (j == 0))
    def _():
        for i in range(2 * units):
            copy(i).start()
        for i in range(2 * units):
            copy(i).wait()
            if i % 2:
                u = i // 2
                weight[:, u * wide : (u + 1) * wide, :] = jnp.swapaxes(raw[u], 0, 1)

    @pl.when(j == 0)
    def _():
        first, second = ids_ref[2 * s], ids_ref[2 * s + 1]

        def product(e):
            full = lax.dot_general(
                cot_ref[...], weight[e], (((1,), (1,)), ((), ())), preferred_element_type=jnp.float32
            )
            return [full[:, i * wide : (i + 1) * wide] for i in range(units)]

        @pl.when(first == second)
        def _():
            for i, part in enumerate(product(first)):
                grad[i] = part

        @pl.when(first != second)
        def _():
            for n, e in enumerate((first, second)):
                for i, part in enumerate(product(e)):
                    grad[i, n * tile : (n + 1) * tile, :] = part[n * tile : (n + 1) * tile]

    for n in range(2):
        of = pl.ds(n * tile, tile)
        live, gate, up, sig = gate_terms(pre_ref.at[of], fill_ref[2 * s + n])
        base = live * grad[j, of, :]
        both = jnp.stack([base * up * sig * (1.0 + gate * (1.0 - sig)), base * (gate * sig)])
        out_ref[of, :, :] = jnp.swapaxes(both.astype(out_ref.dtype), 0, 1)


def input_grads(ids, fill, cols, slots, cot, pre_act, parts, into=None):
    tiles = ids.shape[0]
    rows, width = cot.shape
    pair = 2 * rows // tiles
    two = pre_act.shape[1]
    own, experts, _ = parts[0].shape
    units = len(parts) // 2
    columns = pl.BlockSpec((pair, two, 2 * own), lambda t, j, i, f, c, sl: (t, 0, c[j]))
    anywhere = pl.BlockSpec(memory_space=pl.ANY)
    extra = () if into is None else (into,)
    work = rows * own * units
    return pl.pallas_call(
        functools.partial(grad_kernel, units),
        grid_spec=pltpu.PrefetchScalarGridSpec(
            num_scalar_prefetch=4,
            grid=(tiles // 2, units),
            in_specs=[pl.BlockSpec((pair, width), lambda t, *_: (t, 0)), columns]
            + [anywhere] * (len(parts) + len(extra)),
            out_specs=columns,
            scratch_shapes=[
                pltpu.VMEM((units, 2 * own, experts, width), cot.dtype),
                pltpu.VMEM((experts, units * 2 * own, width), cot.dtype),
                pltpu.VMEM((units, pair, 2 * own), jnp.float32),
                pltpu.SemaphoreType.DMA((len(parts),)),
            ],
        ),
        out_shape=jax.ShapeDtypeStruct(pre_act.shape, pre_act.dtype),
        input_output_aliases={} if into is None else {6 + len(parts): 0},
        compiler_params=params(58),
        cost_estimate=cost(4 * work * width, 2 * (rows * width + 4 * experts * own * units * width + 16 * work)),
        name="input_grads",
    )(ids, fill, cols, slots, cot, pre_act, *parts, *extra)


def body(splits, cotangent, pre_act, down_weight, tile_expert, tile_fill):
    groups, blks = lax.axis_size("group"), lax.axis_size("blk")
    group, blk = lax.axis_index("group"), lax.axis_index("blk")
    hidden = pre_act.shape[2]
    experts, width = down_weight.shape[1:]
    half = width // 2
    owned = hidden // (groups * blks)
    upper = bits_of(blks)[1:]
    zbits = bits_of(groups)
    core = blk & 1
    orders = [upper, upper[::-1]]

    def by_core(pair):
        return jnp.where(core == 0, pair[0], pair[1])

    def across(value, step):
        return lax.ppermute(value, "blk", [(i, i ^ orders[i & 1][step]) for i in range(blks)])

    def swap(value):
        return flip(value, "blk", blks, 1)

    cot2 = swap(cotangent)

    if len(upper) == 2 and groups > 1:
        moves = []
        for g in range(groups):
            for b in range(blks):
                source = (b ^ orders[b & 1][0]) & ~1 | ((b ^ g) & 1)
                moves.append((g * blks + source, g * blks + b))
        straight = lax.ppermute(down_weight, ("group", "blk"), moves)
        round_z = flip(straight, "group", groups, 1)
        far = across(straight, 1)
        own2 = swap(down_weight)
        straight2 = swap(straight)
        round2 = swap(round_z)
        far2 = swap(far)
        near = [by_core([o[0] for o in orders]), by_core([o[1] for o in orders])]
        picked = core ^ (group & 1)
        units = [
            (down_weight, own2, 0, core),
            (straight, round_z, near[0], picked),
            (straight2, round2, near[1], 1 - picked),
            (far, far2, upper[0] ^ upper[1], picked),
        ]
    else:
        held, masks = [down_weight], ([0], [0])
        for step in range(len(upper)):
            held = held + [across(part, step) for part in held]
            masks = tuple(m + [i ^ order[step] for i in m] for m, order in zip(masks, orders))
        units = []
        for i, part in enumerate(held):
            mate = masks[1].index(masks[0][i])
            units.append((part, swap(held[mate]), by_core([m[i] for m in masks]), core))
    cols = jnp.stack([(blk ^ mask) >> 1 for _, _, mask, _ in units]).astype(jnp.int32)
    slots = jnp.stack([s for _, _, _, at in units for s in (at, 1 - at)]).astype(jnp.int32)

    act = activation_t(tile_fill, pre_act)
    act2 = swap(act)
    ids = jnp.concatenate([tile_expert, swap(tile_expert)])
    act_grad = None
    at = 0
    for size in splits:
        parts = [p for unit in units[at : at + size] for p in unit[:2]]
        act_grad = input_grads(
            tile_expert, tile_fill, cols[at : at + size], slots[2 * at : 2 * (at + size)],
            cotangent, pre_act, parts, act_grad,
        )
        at += size

    def granules(step):
        out = []
        for order in orders:
            left = [1] + order[step + 1 :]
            out.append(owned * (1 << sum(1 for m in left if m < order[step])))
        return tuple(out)

    bits = [(blk & by_core([order[step] for order in orders])) != 0 for step in range(len(upper))]
    sizes = [granules(step) for step in range(len(upper))]
    for mask in zbits:
        bits.append((group & mask) != 0)
        sizes.append((2 * owned, 2 * owned))
    bits.append(core != 0)
    sizes.append((owned, owned))
    pos = jnp.stack([core] + [bit.astype(jnp.int32) for bit in bits])

    firsts, counts = (0, half - 768), (half - 768, 768)
    sends, keeps = [], []
    for first, count in zip(firsts, counts):
        send, keep = terms(ids, pos, act, act2, cotangent, cot2, sizes[0], experts, first, count, blks * owned)
        for step in range(len(bits) - 1):
            if step < len(upper):
                recv = across(send, step)
            else:
                recv = flip(send, "group", groups, zbits[step - len(upper)])
            last = step == len(bits) - 2
            send, keep = halve(
                pos, step + 2, keep, recv, sizes[step + 1], jnp.float32 if last else jnp.bfloat16
            )
        sends.append(swap(send))
        keeps.append(keep)
    weight_grad = finish(core.reshape(1), firsts, keeps, sends, (owned, experts, width))
    return act_grad, weight_grad


def solution(mesh):
    placed = (
        P(("group", "blk"), None),
        P(("group", "blk"), None, None),
        P("blk", None, None),
        P(("group", "blk")),
        P(("group", "blk")),
    )
    shape = dict(mesh.shape)
    usual = shape["blk"] == 8 and shape["group"] == 4
    splits = (1, 2, 1) if usual else (1,) * (shape["blk"] // 2)

    def run(*args):
        return body(splits, *args)

    return jax.shard_map(
        run,
        mesh=mesh,
        in_specs=placed,
        out_specs=(P(("group", "blk"), None, None), P(("group", "blk"), None, None)),
        check_vma=False,
    )
```

time: 365 us -> 192 us (0.53)
  waiting for transfers between devices: 210 us -> 79.5 us
  local copies, waits for them, and re-layouts: 94.6 us -> 1.79 us
  Pallas kernels: 0 us -> 82.9 us
  matrix products: 39.4 us -> 0 us
  starting transfers between devices: 0.3 us -> 23.1 us
  between operations: 13.9 us -> 0.79 us
    reduce_scatter x2 -> x0, waiting for transfers between devices: 172 us -> none  [the longest x1 135 us: body(): lax.psum_scatter(jnp.einsum('treh,trd->hed', act_expert, cot_tiles, prefe...]
    pallas_call x0 -> x15, Pallas kernels: none -> 82.9 us  [the longest x3 39.8 us: input_grads(): pl.pallas_call(functools.partial(grad_kernel, units), grid_spec=pltpu.Pre...]
    ppermute x0 -> x20, waiting for transfers between devices: none -> 79.5 us  [the longest x5 55.6 us: across(): lax.ppermute(value, 'blk', [(i, i ^ orders[i & 1][step]) for i in range(b...]
    gather x5 -> x0, local copies, waits for them, and re-layouts: 49.9 us -> none  [body(): chosen = jnp.take(piece, tile_expert, axis=1)]
    dot_general x2 -> x0, matrix products: 39.4 us -> none  [the longest x1 20.2 us: body(): jnp.einsum('trd,ntd->trn', cot_tiles, chosen, preferred_element_type=jnp....]
    all_gather x1 -> x0, waiting for transfers between devices: 37.8 us -> none  [body(): piece = lax.all_gather(down_weight, 'blk', axis=0, tiled=True)]
    unnamed x23 -> x10, local copies, waits for them, and re-layouts: 27.7 us -> 1.17 us
    ppermute x0 -> x20, starting transfers between devices: none -> 23.1 us  [the longest x5 10.3 us: across(): lax.ppermute(value, 'blk', [(i, i ^ orders[i & 1][step]) for i in range(b...]
  transfers between devices with their start and end apart: 3 -> 20, of which waited for: 3 -> 8; matrix products, arithmetic and copies ran while one was open for 36% -> 2% of each run, Pallas kernels for 0% -> 43%
where the time goes in v1:
time: 192 us; the launch traced here: 191 us
  Pallas kernels  82.9 us (43%)
  waiting for transfers between devices  79.5 us (41%)
  starting transfers between devices  23.1 us (12%)
  other arithmetic  3.03 us (2%)
    ppermute x5, waiting for transfers between devices, across(): lax.ppermute(value, 'blk', [(i, i ^ orders[i & 1][step]) for i in range(b...  55.6 us
    pallas_call x3, Pallas kernels, input_grads(): pl.pallas_call(functools.partial(grad_kernel, units), grid_spec=pltpu.Pre...  39.8 us
    pallas_call x2, Pallas kernels, terms(): pl.pallas_call(functools.partial(term_kernel, granules, first, count, til...  26.6 us
    ppermute x14, waiting for transfers between devices, flip(): return lax.ppermute(value, axis, [(i, i ^ mask) for i in range(size)])  21.6 us
    ppermute x5, starting transfers between devices, across(): lax.ppermute(value, 'blk', [(i, i ^ orders[i & 1][step]) for i in range(b...  10.3 us
    ppermute x14, starting transfers between devices, flip(): return lax.ppermute(value, axis, [(i, i ^ mask) for i in range(size)])  9.85 us
    pallas_call x8, Pallas kernels, halve(): pl.pallas_call(functools.partial(step_kernel, granules, step), in_specs=[...  8.65 us
    pallas_call x1, Pallas kernels, activation_t(): pl.pallas_call(activation_kernel, grid_spec=pltpu.PrefetchScalarGridSpec(...  6.74 us
  transfers between devices with their start and end apart: 20, of which 8 were waited for; matrix products, arithmetic and copies ran while one was open for 2% of the time, Pallas kernels for 43%

profile of v1, /device:TPU:0, one launch (start us, length us, event | category | flops | bytes accessed | tf_op | source)
XLA Modules:
  0.0 191.2 jit_solution(6212820006106783081)
XLA Ops:
  1.2 6.7 %activation_t.1.own_ref = bf16[1024,768]{1,0:T(8,128)(2,1)} custom-call(s32[6]{0:T(128)} %fill_ref.7, bf16[768,2,1024]{2,1,0:T(2,128)(2,1)} %pre_ref.7), custom_call_target="tpu_custom_call" | custom-call | bytes 4718592 | tf_op jit(solution)/shard_map/activation_t/pallas_call | solution.py:49
  8.0 3.0 %collective-permute-start = (bf16[128,2,3584]{2,1,0:T(2,128)(2,1)}, bf16[128,2,3584]{2,1,0:T(2,128)(2,1)}, u32[]{:S(2)}, u32[]{:S(2)}) collective-permute-start(bf16[128,2,3584]{2,1,0:T(2,128)(2,1)} %refs_0_.1), channel_id=1, source_target_pairs={{2,0},{5,1},{0,2},{7,3},{6,4},{1,5},{4,6},{3,7},{11,8},{12,9},{9,1... | collective-permute-start | bytes 5505032 | tf_op jit(solution)/shard_map/ppermute | solution.py:303
  11.6 0.8 collective-permute-done.7
  12.9 1.1 copy-done.4
  14.1 13.2 %terms.2 = (bf16[2,512,1024]{2,1,0:T(8,128)(2,1)}, f32[2,512,1024]{2,1,0:T(8,128)}) custom-call(s32[12]{0:T(128)} %pad_add_fusion.4.ids_ref, s32[6]{0:T(128)} %stack.94.pos_ref, bf16[1024,768]{1,0:T(8,128)(2,1)} %activation_t.1.own_ref, bf16[1024,768]{1,0:T(8,128)(2,1)} %copy-done.4, bf16[768,3584]{1,0:T(8,128)(2,1)} %cot_ref.9, ...), custom_call_target="tpu_custom_call" | custom-call | flops 6442450944 | bytes 23592960 | tf_op jit(solution)/shard_map/terms/pallas_call | solution.py:106
  27.2 2.8 %collective-permute-start.10 = (bf16[2,512,1024]{2,1,0:T(8,128)(2,1)}, bf16[2,512,1024]{2,1,0:T(8,128)(2,1)}, u32[]{:S(2)}, u32[]{:S(2)}) collective-permute-start(bf16[2,512,1024]{2,1,0:T(8,128)(2,1)} %get-tuple-element.23), channel_id=1, source_target_pairs={{0,2},{1,5},{2,0},{3,7},{4,6},{5,1},{6,4},{7,3},{8,10},{9,13},{10,... | collective-permute-start | bytes 6291464 | tf_op jit(solution)/shard_map/ppermute | solution.py:290
  30.1 2.4 %collective-permute-done.refs_0_ = bf16[128,2,3584]{2,1,0:T(2,128)(2,1)} collective-permute-done((bf16[128,2,3584]{2,1,0:T(2,128)(2,1)}, bf16[128,2,3584]{2,1,0:T(2,128)(2,1)}, u32[]{:S(2)}, u32[]{:S(2)}) %collective-permute-start) | collective-permute-done | bytes 1835040 | tf_op jit(solution)/shard_map/ppermute | solution.py:303
  32.4 1.8 collective-permute-start.3
  34.2 1.3 collective-permute-start.1
  35.5 13.4 %terms.3 = (bf16[2,512,768]{2,1,0:T(8,128)(2,1)}, f32[2,512,768]{2,1,0:T(8,128)}) custom-call(s32[12]{0:T(128)} %pad_add_fusion.4.ids_ref, s32[6]{0:T(128)} %stack.94.pos_ref, bf16[1024,768]{1,0:T(8,128)(2,1)} %activation_t.1.own_ref, bf16[1024,768]{1,0:T(8,128)(2,1)} %copy-done.4, bf16[768,3584]{1,0:T(8,128)(2,1)} %cot_ref.9, ...), custom_call_target="tpu_custom_call" | custom-call | flops 4831838208 | bytes 20447232 | tf_op jit(solution)/shard_map/terms/pallas_call | solution.py:106
  48.9 1.5 collective-permute-start.14
  50.4 21.6 %collective-permute-done.10.recv_ref = bf16[2,512,1024]{2,1,0:T(8,128)(2,1)} collective-permute-done((bf16[2,512,1024]{2,1,0:T(8,128)(2,1)}, bf16[2,512,1024]{2,1,0:T(8,128)(2,1)}, u32[]{:S(2)}, u32[]{:S(2)}) %collective-permute-start.10) | collective-permute-done | bytes 2097184 | tf_op jit(solution)/shard_map/ppermute | solution.py:290
  72.0 2.5 %halve.8 = (bf16[2,256,1024]{2,1,0:T(8,128)(2,1)S(1)}, f32[2,256,1024]{2,1,0:T(8,128)S(1)}) custom-call(s32[6]{0:T(128)S(1)} %copy-done.2, f32[2,512,1024]{2,1,0:T(8,128)S(1)} %copy-done, bf16[2,512,1024]{2,1,0:T(8,128)(2,1)} %collective-permute-done.10.recv_ref), custom_call_target="tpu_custom_call" | custom-call | bytes 9437184 | tf_op jit(solution)/shard_map/halve/pallas_call | solution.py:144
  74.5 2.6 %collective-permute-start.11 = (bf16[2,256,1024]{2,1,0:T(8,128)(2,1)S(1)}, bf16[2,256,1024]{2,1,0:T(8,128)(2,1)S(1)}, u32[]{:S(2)}, u32[]{:S(2)}) collective-permute-start(bf16[2,256,1024]{2,1,0:T(8,128)(2,1)S(1)} %get-tuple-element.25), channel_id=1, source_target_pairs={{0,4},{1,3},{2,6},{3,1},{4,0},{5,7},{6,2},{7,5},{8,12},{9,11},{10,... | collective-permute-start | bytes 3145736 | tf_op jit(solution)/shard_map/ppermute | solution.py:290
  77.0 25.5 %collective-permute-done.14.recv_ref = bf16[2,512,768]{2,1,0:T(8,128)(2,1)S(1)} collective-permute-done((bf16[2,512,768]{2,1,0:T(8,128)(2,1)}, bf16[2,512,768]{2,1,0:T(8,128)(2,1)S(1)}, u32[]{:S(2)}, u32[]{:S(2)}) %collective-permute-start.14) | collective-permute-done | bytes 1572896 | tf_op jit(solution)/shard_map/ppermute | solution.py:290
  102.6 1.1 halve.12
  103.7 2.1 %collective-permute-start.15 = (bf16[2,256,768]{2,1,0:T(8,128)(2,1)S(1)}, bf16[2,256,768]{2,1,0:T(8,128)(2,1)S(1)}, u32[]{:S(2)}, u32[]{:S(2)}) collective-permute-start(bf16[2,256,768]{2,1,0:T(8,128)(2,1)S(1)} %get-tuple-element.34), channel_id=1, source_target_pairs={{0,4},{1,3},{2,6},{3,1},{4,0},{5,7},{6,2},{7,5},{8,12},{9,11},{10,... | collective-permute-start | bytes 2359304 | tf_op jit(solution)/shard_map/ppermute | solution.py:290
  106.4 0.9 halve.9
  107.3 8.5 %collective-permute-done.15.recv_ref = bf16[2,256,768]{2,1,0:T(8,128)(2,1)S(1)} collective-permute-done((bf16[2,256,768]{2,1,0:T(8,128)(2,1)S(1)}, bf16[2,256,768]{2,1,0:T(8,128)(2,1)S(1)}, u32[]{:S(2)}, u32[]{:S(2)}) %collective-permute-start.15) | collective-permute-done | bytes 786464 | tf_op jit(solution)/shard_map/ppermute | solution.py:290
  115.8 1.6 collective-permute-start.12
  117.3 1.6 halve.13
  118.9 9.8 %collective-permute-done.12.recv_ref = bf16[2,128,1024]{2,1,0:T(8,128)(2,1)S(1)} collective-permute-done((bf16[2,128,1024]{2,1,0:T(8,128)(2,1)S(1)}, bf16[2,128,1024]{2,1,0:T(8,128)(2,1)S(1)}, u32[]{:S(2)}, u32[]{:S(2)}) %collective-permute-start.12) | collective-permute-done | bytes 524320 | tf_op jit(solution)/shard_map/ppermute | solution.py:20
  128.7 1.7 collective-permute-start.16
  131.1 0.7 pad_add_fusion.slot_ref
  131.7 0.7 halve.10
  132.5 5.9 %collective-permute-done.16.recv_ref = bf16[2,128,768]{2,1,0:T(8,128)(2,1)S(1)} collective-permute-done((bf16[2,128,768]{2,1,0:T(8,128)(2,1)}, bf16[2,128,768]{2,1,0:T(8,128)(2,1)S(1)}, u32[]{:S(2)}, u32[]{:S(2)}) %collective-permute-start.16) | collective-permute-done | bytes 393248 | tf_op jit(solution)/shard_map/ppermute | solution.py:20
  138.3 2.6 %collective-permute-start.13 = (bf16[2,64,1024]{2,1,0:T(8,128)(2,1)S(1)}, bf16[2,64,1024]{2,1,0:T(8,128)(2,1)S(1)}, u32[]{:S(2)}, u32[]{:S(2)}) collective-permute-start(bf16[2,64,1024]{2,1,0:T(8,128)(2,1)S(1)} %get-tuple-element.29), channel_id=1, source_target_pairs={{0,16},{8,24},{16,0},{24,8},{1,17},{9,25},{17,1},{25,9},{2,18},{10... | collective-permute-start | bytes 786440 | tf_op jit(solution)/shard_map/ppermute | solution.py:20
  143.1 10.7 %input_grads.3.refs_4_ = bf16[768,2,1024]{2,1,0:T(2,128)(2,1)} custom-call(s32[6]{0:T(128)} %ids_ref.5, s32[6]{0:T(128)} %fill_ref.7, s32[1]{0:T(128)} %bitcast.5.col_ref, s32[2]{0:T(128)} %pad_add_fusion.3.slot_ref, bf16[768,3584]{1,0:T(8,128)(2,1)} %cot_ref.9, bf16[768,2,1024]{2,1,0:T(2,128)(2,1)} %pre_ref.7, bf16[128,2,3584]{2,1,0:T(2,128)(2,1)} %refs_0_.1, ...), custom_call_target="tpu_custom_call" | custom-call | flops 1409286144 | bytes 15990784 | tf_op jit(solution)/shard_map/input_grads/pallas_call | solution.py:251
  153.9 5.2 %collective-permute-done.17.recv_ref = bf16[2,64,768]{2,1,0:T(8,128)(2,1)S(1)} collective-permute-done((bf16[2,64,768]{2,1,0:T(8,128)(2,1)S(1)}, bf16[2,64,768]{2,1,0:T(8,128)(2,1)S(1)}, u32[]{:S(2)}, u32[]{:S(2)}) %collective-permute-start.17) | collective-permute-done | bytes 196640 | tf_op jit(solution)/shard_map/ppermute | solution.py:20
  160.9 18.3 %input_grads.4.refs_2_ = bf16[768,2,1024]{2,1,0:T(2,128)(2,1)} custom-call(s32[6]{0:T(128)} %ids_ref.5, s32[6]{0:T(128)} %fill_ref.7, s32[2]{0:T(128)} %pad_add_fusion.1.col_ref, s32[4]{0:T(128)} %pad_add_fusion.2.slot_ref, bf16[768,3584]{1,0:T(8,128)(2,1)} %cot_ref.9, bf16[768,2,1024]{2,1,0:T(2,128)(2,1)} %pre_ref.7, ...), custom_call_target="tpu_custom_call", output_to_operand_aliasing={{}: (10, {})} | custom-call | flops 2818572288 | bytes 26476544 | tf_op jit(solution)/shard_map/input_grads/pallas_call | solution.py:251
  179.2 10.7 %input_grads.5 = bf16[768,2,1024]{2,1,0:T(2,128)(2,1)} custom-call(s32[6]{0:T(128)} %ids_ref.5, s32[6]{0:T(128)} %fill_ref.7, s32[1]{0:T(128)} %bitcast.col_ref, s32[2]{0:T(128)} %pad_add_fusion.slot_ref, bf16[768,3584]{1,0:T(8,128)(2,1)} %cot_ref.9, bf16[768,2,1024]{2,1,0:T(2,128)(2,1)} %pre_ref.7, ...), custom_call_target="tpu_custom_call", output_to_operand_aliasing={{}: (8, {})} | custom-call | flops 1409286144 | bytes 15990784 | tf_op jit(solution)/shard_map/input_grads/pallas_call | solution.py:251
  190.0 1.1 finish.1
  (39 shorter events, 7.1 us)
Async XLA Ops:
  0.6 10.3 %copy-start.3 = (s32[6]{0:T(128)S(1)}, s32[6]{0:T(128)}, u32[]{:S(2)}) copy-start(s32[6]{0:T(128)} %ids_ref.5) | copy-start | bytes 76
  0.6 12.3 %collective-permute-start.9 = (bf16[768,3584]{1,0:T(8,128)(2,1)}, bf16[768,3584]{1,0:T(8,128)(2,1)}, u32[]{:S(2)}, u32[]{:S(2)}) collective-permute-start(bf16[768,3584]{1,0:T(8,128)(2,1)} %cot_ref.9), channel_id=1, source_target_pairs={{0,1},{1,0},{2,3},{3,2},{4,5},{5,4},{6,7},{7,6},{8,9},{9,8},{10,11... | collective-permute-start | bytes 16515080 | tf_op jit(solution)/shard_map/ppermute | solution.py:20
  7.9 5.0 %collective-permute-start.8 = (bf16[1024,768]{1,0:T(8,128)(2,1)}, bf16[1024,768]{1,0:T(8,128)(2,1)S(1)}, u32[]{:S(2)}, u32[]{:S(2)}) collective-permute-start(bf16[1024,768]{1,0:T(8,128)(2,1)} %activation_t.1.own_ref), channel_id=1, source_target_pairs={{0,1},{1,0},{2,3},{3,2},{4,5},{5,4},{6,7},{7,6},{8,9},{9,8},{10,11... | collective-permute-start | bytes 4718600 | tf_op jit(solution)/shard_map/ppermute | solution.py:20
  8.0 24.5 %collective-permute-start = (bf16[128,2,3584]{2,1,0:T(2,128)(2,1)}, bf16[128,2,3584]{2,1,0:T(2,128)(2,1)}, u32[]{:S(2)}, u32[]{:S(2)}) collective-permute-start(bf16[128,2,3584]{2,1,0:T(2,128)(2,1)} %refs_0_.1), channel_id=1, source_target_pairs={{2,0},{5,1},{0,2},{7,3},{6,4},{1,5},{4,6},{3,7},{11,8},{12,9},{9,1... | collective-permute-start | bytes 5505032 | tf_op jit(solution)/shard_map/ppermute | solution.py:303
  10.9 1.4 collective-permute-start.7
  12.9 1.2 copy-start.4
  27.2 44.8 %copy-start.2 = (s32[6]{0:T(128)S(1)}, s32[6]{0:T(128)}, u32[]{:S(2)}) copy-start(s32[6]{0:T(128)} %stack.94.pos_ref) | copy-start | bytes 76
  27.2 44.8 %collective-permute-start.10 = (bf16[2,512,1024]{2,1,0:T(8,128)(2,1)}, bf16[2,512,1024]{2,1,0:T(8,128)(2,1)}, u32[]{:S(2)}, u32[]{:S(2)}) collective-permute-start(bf16[2,512,1024]{2,1,0:T(8,128)(2,1)} %get-tuple-element.23), channel_id=1, source_target_pairs={{0,2},{1,5},{2,0},{3,7},{4,6},{5,1},{6,4},{7,3},{8,10},{9,13},{10,... | collective-permute-start | bytes 6291464 | tf_op jit(solution)/shard_map/ppermute | solution.py:290
  32.4 73.3 %collective-permute-start.3 = (bf16[128,2,3584]{2,1,0:T(2,128)(2,1)}, bf16[128,2,3584]{2,1,0:T(2,128)(2,1)}, u32[]{:S(2)}, u32[]{:S(2)}) collective-permute-start(bf16[128,2,3584]{2,1,0:T(2,128)(2,1)} %collective-permute-done.refs_0_), channel_id=1, source_target_pairs={{0,8},{8,0},{16,24},{24,16},{1,9},{9,1},{17,25},{25,17},{2,10},{10... | collective-permute-start | bytes 5505032 | tf_op jit(solution)/shard_map/ppermute | solution.py:20
  34.2 71.6 %collective-permute-start.1 = (bf16[128,2,3584]{2,1,0:T(2,128)(2,1)}, bf16[128,2,3584]{2,1,0:T(2,128)(2,1)}, u32[]{:S(2)}, u32[]{:S(2)}) collective-permute-start(bf16[128,2,3584]{2,1,0:T(2,128)(2,1)} %collective-permute-done.refs_0_), channel_id=1, source_target_pairs={{0,4},{1,3},{2,6},{3,1},{4,0},{5,7},{6,2},{7,5},{8,12},{9,11},{10,... | collective-permute-start | bytes 5505032 | tf_op jit(solution)/shard_map/ppermute | solution.py:290
  35.5 36.5 %copy-start = (f32[2,512,1024]{2,1,0:T(8,128)S(1)}, f32[2,512,1024]{2,1,0:T(8,128)}, u32[]{:S(2)}) copy-start(f32[2,512,1024]{2,1,0:T(8,128)} %get-tuple-element.22.keep_ref) | copy-start | bytes 12582916
  48.9 53.6 %collective-permute-start.14 = (bf16[2,512,768]{2,1,0:T(8,128)(2,1)}, bf16[2,512,768]{2,1,0:T(8,128)(2,1)S(1)}, u32[]{:S(2)}, u32[]{:S(2)}) collective-permute-start(bf16[2,512,768]{2,1,0:T(8,128)(2,1)} %get-tuple-element.32), channel_id=1, source_target_pairs={{0,2},{1,5},{2,0},{3,7},{4,6},{5,1},{6,4},{7,3},{8,10},{9,13},{10,... | collective-permute-start | bytes 4718600 | tf_op jit(solution)/shard_map/ppermute | solution.py:290
  72.0 30.6 %copy-start.1 = (f32[2,512,768]{2,1,0:T(8,128)S(1)}, f32[2,512,768]{2,1,0:T(8,128)}, u32[]{:S(2)}) copy-start(f32[2,512,768]{2,1,0:T(8,128)} %get-tuple-element.31.keep_ref) | copy-start | bytes 9437188
  74.5 31.8 %collective-permute-start.11 = (bf16[2,256,1024]{2,1,0:T(8,128)(2,1)S(1)}, bf16[2,256,1024]{2,1,0:T(8,128)(2,1)S(1)}, u32[]{:S(2)}, u32[]{:S(2)}) collective-permute-start(bf16[2,256,1024]{2,1,0:T(8,128)(2,1)S(1)} %get-tuple-element.25), channel_id=1, source_target_pairs={{0,4},{1,3},{2,6},{3,1},{4,0},{5,7},{6,2},{7,5},{8,12},{9,11},{10,... | collective-permute-start | bytes 3145736 | tf_op jit(solution)/shard_map/ppermute | solution.py:290
  77.0 65.1 %collective-permute-start.6 = (bf16[128,2,3584]{2,1,0:T(2,128)(2,1)}, bf16[128,2,3584]{2,1,0:T(2,128)(2,1)}, u32[]{:S(2)}, u32[]{:S(2)}) collective-permute-start(bf16[128,2,3584]{2,1,0:T(2,128)(2,1)} %refs_0_.1), channel_id=1, source_target_pairs={{0,1},{1,0},{2,3},{3,2},{4,5},{5,4},{6,7},{7,6},{8,9},{9,8},{10,11... | collective-permute-start | bytes 5505032 | tf_op jit(solution)/shard_map/ppermute | solution.py:20
  103.7 12.1 %collective-permute-start.15 = (bf16[2,256,768]{2,1,0:T(8,128)(2,1)S(1)}, bf16[2,256,768]{2,1,0:T(8,128)(2,1)S(1)}, u32[]{:S(2)}, u32[]{:S(2)}) collective-permute-start(bf16[2,256,768]{2,1,0:T(8,128)(2,1)S(1)} %get-tuple-element.34), channel_id=1, source_target_pairs={{0,4},{1,3},{2,6},{3,1},{4,0},{5,7},{6,2},{7,5},{8,12},{9,11},{10,... | collective-permute-start | bytes 2359304 | tf_op jit(solution)/shard_map/ppermute | solution.py:290
  105.8 55.1 %collective-permute-start.4 = (bf16[128,2,3584]{2,1,0:T(2,128)(2,1)}, bf16[128,2,3584]{2,1,0:T(2,128)(2,1)}, u32[]{:S(2)}, u32[]{:S(2)}) collective-permute-start(bf16[128,2,3584]{2,1,0:T(2,128)(2,1)} %collective-permute-done.refs_0_), channel_id=1, source_target_pairs={{0,1},{1,0},{2,3},{3,2},{4,5},{5,4},{6,7},{7,6},{8,9},{9,8},{10,11... | collective-permute-start | bytes 5505032 | tf_op jit(solution)/shard_map/ppermute | solution.py:20
  105.8 55.1 %collective-permute-start.5 = (bf16[128,2,3584]{2,1,0:T(2,128)(2,1)}, bf16[128,2,3584]{2,1,0:T(2,128)(2,1)}, u32[]{:S(2)}, u32[]{:S(2)}) collective-permute-start(bf16[128,2,3584]{2,1,0:T(2,128)(2,1)} %collective-permute-done.3.refs_1_), channel_id=1, source_target_pairs={{0,1},{1,0},{2,3},{3,2},{4,5},{5,4},{6,7},{7,6},{8,9},{9,8},{10,11... | collective-permute-start | bytes 5505032 | tf_op jit(solution)/shard_map/ppermute | solution.py:20
  106.3 72.9 %collective-permute-start.2 = (bf16[128,2,3584]{2,1,0:T(2,128)(2,1)}, bf16[128,2,3584]{2,1,0:T(2,128)(2,1)}, u32[]{:S(2)}, u32[]{:S(2)}) collective-permute-start(bf16[128,2,3584]{2,1,0:T(2,128)(2,1)} %collective-permute-done.1.refs_0_), channel_id=1, source_target_pairs={{0,1},{1,0},{2,3},{3,2},{4,5},{5,4},{6,7},{7,6},{8,9},{9,8},{10,11... | collective-permute-start | bytes 5505032 | tf_op jit(solution)/shard_map/ppermute | solution.py:20
  115.8 12.9 %collective-permute-start.12 = (bf16[2,128,1024]{2,1,0:T(8,128)(2,1)S(1)}, bf16[2,128,1024]{2,1,0:T(8,128)(2,1)S(1)}, u32[]{:S(2)}, u32[]{:S(2)}) collective-permute-start(bf16[2,128,1024]{2,1,0:T(8,128)(2,1)S(1)} %get-tuple-element.27), channel_id=1, source_target_pairs={{0,8},{8,0},{16,24},{24,16},{1,9},{9,1},{17,25},{25,17},{2,10},{10... | collective-permute-start | bytes 1572872 | tf_op jit(solution)/shard_map/ppermute | solution.py:20
  128.7 9.6 %collective-permute-start.16 = (bf16[2,128,768]{2,1,0:T(8,128)(2,1)}, bf16[2,128,768]{2,1,0:T(8,128)(2,1)S(1)}, u32[]{:S(2)}, u32[]{:S(2)}) collective-permute-start(bf16[2,128,768]{2,1,0:T(8,128)(2,1)} %get-tuple-element.36), channel_id=1, source_target_pairs={{0,8},{8,0},{16,24},{24,16},{1,9},{9,1},{17,25},{25,17},{2,10},{10... | collective-permute-start | bytes 1179656 | tf_op jit(solution)/shard_map/ppermute | solution.py:20
  138.3 21.4 %collective-permute-start.13 = (bf16[2,64,1024]{2,1,0:T(8,128)(2,1)S(1)}, bf16[2,64,1024]{2,1,0:T(8,128)(2,1)S(1)}, u32[]{:S(2)}, u32[]{:S(2)}) collective-permute-start(bf16[2,64,1024]{2,1,0:T(8,128)(2,1)S(1)} %get-tuple-element.29), channel_id=1, source_target_pairs={{0,16},{8,24},{16,0},{24,8},{1,17},{9,25},{17,1},{25,9},{2,18},{10... | collective-permute-start | bytes 786440 | tf_op jit(solution)/shard_map/ppermute | solution.py:20
  142.2 16.9 %collective-permute-start.17 = (bf16[2,64,768]{2,1,0:T(8,128)(2,1)S(1)}, bf16[2,64,768]{2,1,0:T(8,128)(2,1)S(1)}, u32[]{:S(2)}, u32[]{:S(2)}) collective-permute-start(bf16[2,64,768]{2,1,0:T(8,128)(2,1)S(1)} %get-tuple-element.38), channel_id=1, source_target_pairs={{0,16},{8,24},{16,0},{24,8},{1,17},{9,25},{17,1},{25,9},{2,18},{10... | collective-permute-start | bytes 589832 | tf_op jit(solution)/shard_map/ppermute | solution.py:20
  159.6 30.4 %collective-permute-start.19 = (f32[2,32,768]{2,1,0:T(8,128)S(1)}, f32[2,32,768]{2,1,0:T(8,128)S(1)}, u32[]{:S(2)}, u32[]{:S(2)}) collective-permute-start(f32[2,32,768]{2,1,0:T(8,128)S(1)} %get-tuple-element.41), channel_id=1, source_target_pairs={{0,1},{1,0},{2,3},{3,2},{4,5},{5,4},{6,7},{7,6},{8,9},{9,8},{10,11... | collective-permute-start | bytes 589832 | tf_op jit(solution)/shard_map/ppermute | solution.py:20
  160.4 29.6 %collective-permute-start.18 = (f32[2,32,1024]{2,1,0:T(8,128)S(1)}, f32[2,32,1024]{2,1,0:T(8,128)S(1)}, u32[]{:S(2)}, u32[]{:S(2)}) collective-permute-start(f32[2,32,1024]{2,1,0:T(8,128)S(1)} %get-tuple-element.40), channel_id=1, source_target_pairs={{0,1},{1,0},{2,3},{3,2},{4,5},{5,4},{6,7},{7,6},{8,9},{9,8},{10,11... | collective-permute-start | bytes 786440 | tf_op jit(solution)/shard_map/ppermute | solution.py:20

commit v2 on v1

--- a/solution.py
+++ b/solution.py
@@ -37,25 +37,29 @@
     return live, gate, up, sig
 
 
-def activation_kernel(fill_ref, pre_ref, out_ref):
-    live, gate, up, sig = gate_terms(pre_ref, fill_ref[pl.program_id(0)])
-    out_ref[...] = (live * (gate * sig) * up).T.astype(out_ref.dtype)
+def activation_kernel(tile, fill_ref, pre_ref, out_ref):
+    count = pre_ref.shape[0] // tile
+    for n in range(count):
+        of = pl.ds(n * tile, tile)
+        live, gate, up, sig = gate_terms(pre_ref.at[of], fill_ref[count * pl.program_id(0) + n])
+        out_ref[:, of] = (live * (gate * sig) * up).astype(out_ref.dtype).T
 
 
 def activation_t(tile_fill, pre_act):
     tiles = tile_fill.shape[0]
     rows, two, hidden = pre_act.shape
     tile = rows // tiles
+    block = 2 * tile
     return pl.pallas_call(
-        activation_kernel,
+        functools.partial(activation_kernel, tile),
         grid_spec=pltpu.PrefetchScalarGridSpec(
             num_scalar_prefetch=1,
-            grid=(tiles,),
-            in_specs=[pl.BlockSpec((tile, two, hidden), lambda t, f: (t, 0, 0))],
-            out_specs=pl.BlockSpec((hidden, tile), lambda t, f: (0, t)),
+            grid=(rows // block,),
+            in_specs=[pl.BlockSpec((block, two, hidden), lambda t, f: (t, 0, 0))],
+            out_specs=pl.BlockSpec((hidden, block), lambda t, f: (0, t)),
         ),
         out_shape=jax.ShapeDtypeStruct((hidden, rows), pre_act.dtype),
-        compiler_params=params(58),
+        compiler_params=params(32),
         cost_estimate=cost(0, 6 * rows * hidden),
         name="activation_t",
     )(tile_fill, pre_act)
@@ -75,56 +79,96 @@
             pl.when(core_ref == core)(functools.partial(blocks, granules[core]))
 
 
-def term_kernel(granules, first, count, tiles, ids_ref, pos_ref, own_ref, other_ref, cot_ref, cot2_ref, send, keep, acc):
-    tile = own_ref.shape[1] // tiles
-
-    def masked(act_ref, start, e):
-        parts = []
-        for t in range(tiles):
-            part = act_ref[:, t * tile : (t + 1) * tile]
-            parts.append(jnp.where(ids_ref[start + t] == e, part, jnp.zeros_like(part)))
-        return jnp.concatenate(parts, axis=1)
-
-    for e in range(send.shape[0]):
-        acc[...] = jnp.dot(
-            masked(own_ref, 0, e), cot_ref[:, first : first + count], preferred_element_type=jnp.float32
-        ) + jnp.dot(
-            masked(other_ref, tiles, e), cot2_ref[:, first : first + count], preferred_element_type=jnp.float32
-        )
-
-        def move(to, kept, sent):
-            keep[e, to, :] = acc[kept, :]
-            send[e, to, :] = acc[sent, :].astype(send.dtype)
-
-        part_rows(pos_ref[0], pos_ref[1], acc.shape[0], granules, move)
-
-
-def terms(ids, pos, own_t, other_t, cot, cot2, granules, experts, first, count, block):
-    hidden, rows = own_t.shape
-    half = cot.shape[1] // 2
-    tiles = ids.shape[0] // 2
+def load_terms(kind, first, granules, ids_ref, pos_ref, act_hbm, cot_hbm, act, masked, cot, act_sem, cot_sem):
+    hidden, rows = act.shape[1:]
+    tiles = ids_ref[0].shape[0]
+    tile = rows // tiles
+    e = pl.program_id(0)
+
+    def act_copy(n):
+        return pltpu.make_async_copy(act_hbm[n], act.at[n], act_sem.at[n])
+
+    def cot_copy(n):
+        half = cot_hbm[n].shape[1] // 2
+        columns = pl.ds(pl.multiple_of(pos_ref[0] * half + first, 128), cot.shape[1])
+        return pltpu.make_async_copy(cot_hbm[n].at[:, columns], cot.at[pl.ds(n * rows, rows)], cot_sem.at[n])
+
+    @pl.when(e == 0)
+    def _():
+        for n in range(2):
+            act_copy(n).start()
+        for n in range(2):
+            cot_copy(n).start()
+        for n in range(2):
+            act_copy(n).wait()
+
+    def move(to, kept, sent):
+        of = kept if kind else sent
+        for n in range(2):
+            for t in range(tiles):
+                part = act[n, of, t * tile : (t + 1) * tile]
+                at = n * rows + t * tile
+                masked[to, at : at + tile] = jnp.where(ids_ref[n][t] == e, part, jnp.zeros_like(part))
+
+    part_rows(pos_ref[0], pos_ref[1], hidden, granules, move)
+
+    @pl.when(e == 0)
+    def _():
+        for n in range(2):
+            cot_copy(n).wait()
+
+
+def sent_kernel(first, granules, ids_ref, ids2_ref, pos_ref, own_ref, other_ref, cot_ref, cot2_ref, send, *scratch):
+    masked, cot = scratch[1:3]
+    load_terms(0, first, granules, (ids_ref, ids2_ref), pos_ref, (own_ref, other_ref), (cot_ref, cot2_ref), *scratch)
+    send[0] = jnp.dot(masked[...], cot[...], preferred_element_type=jnp.float32).astype(send.dtype)
+
+
+def kept_kernel(first, granules, following, ids_ref, ids2_ref, pos_ref, own_ref, other_ref, cot_ref, cot2_ref, recv, send, keep, acc, *scratch):
+    masked, cot = scratch[1:3]
+    load_terms(1, first, granules, (ids_ref, ids2_ref), pos_ref, (own_ref, other_ref), (cot_ref, cot2_ref), *scratch)
+    acc[...] = recv[0].astype(jnp.float32) + jnp.dot(masked[...], cot[...], preferred_element_type=jnp.float32)
+
+    def move(to, kept, sent):
+        keep[0, to, :] = acc[kept, :]
+        send[0, to, :] = acc[sent, :].astype(send.dtype)
+
+    part_rows(pos_ref[0], pos_ref[2], acc.shape[0], following, move)
+
+
+def terms(kernel, sources, count, experts, recv=()):
+    hidden, rows = sources[3].shape
+    anywhere = pl.BlockSpec(memory_space=pl.ANY)
+    dma = pltpu.SemaphoreType.DMA
+
+    def spec(part):
+        return pl.BlockSpec((1, hidden // part, count), lambda e, *_: (e, 0, 0))
+
+    if recv:
+        kinds = ((4, jnp.bfloat16), (4, jnp.float32))
+    else:
+        kinds = ((2, jnp.bfloat16),)
     return pl.pallas_call(
-        functools.partial(term_kernel, granules, first, count, tiles),
+        kernel,
         grid_spec=pltpu.PrefetchScalarGridSpec(
-            num_scalar_prefetch=2,
-            grid=(hidden // block,),
-            in_specs=[
-                pl.BlockSpec((block, rows), lambda g, i, p: (g, 0)),
-                pl.BlockSpec((block, rows), lambda g, i, p: (g, 0)),
-                pl.BlockSpec((rows, half), lambda g, i, p: (0, p[0])),
-                pl.BlockSpec((rows, half), lambda g, i, p: (0, p[0])),
+            num_scalar_prefetch=3,
+            grid=(experts,),
+            in_specs=[anywhere] * 4 + [spec(2)] * len(recv),
+            out_specs=[spec(part) for part, _ in kinds],
+            scratch_shapes=[pltpu.VMEM((hidden // 2, count), jnp.float32)] * len(recv)
+            + [
+                pltpu.VMEM((2, hidden, rows), jnp.bfloat16),
+                pltpu.VMEM((hidden // 2, 2 * rows), jnp.bfloat16),
+                pltpu.VMEM((2 * rows, count), jnp.bfloat16),
+                dma((2,)),
+                dma((2,)),
             ],
-            out_specs=[pl.BlockSpec((experts, block // 2, count), lambda g, i, p: (0, g, 0))] * 2,
-            scratch_shapes=[pltpu.VMEM((block, count), jnp.float32)],
         ),
-        out_shape=[
-            jax.ShapeDtypeStruct((experts, hidden // 2, count), jnp.bfloat16),
-            jax.ShapeDtypeStruct((experts, hidden // 2, count), jnp.float32),
-        ],
-        compiler_params=params(58),
-        cost_estimate=cost(4 * hidden * 2 * rows * count, 12 * hidden * count + 8 * rows * half),
+        out_shape=[jax.ShapeDtypeStruct((experts, hidden // part, count), kind) for part, kind in kinds],
+        compiler_params=params(32),
+        cost_estimate=cost(2 * hidden * 2 * rows * count, 6 * hidden * count + 8 * rows * count),
         name="terms",
-    )(ids, pos, own_t, other_t, cot, cot2)
+    )(*sources, *recv)
 
 
 def step_kernel(granules, step, pos_ref, keep_ref, recv_ref, *refs):
@@ -186,89 +230,105 @@
     )(core, *keeps, *others)
 
 
-def grad_kernel(units, ids_ref, fill_ref, col_ref, slot_ref, cot_ref, pre_ref, *refs):
+def grad_kernel(at, units, ids_ref, fill_ref, where_ref, cot_hbm, pre_hbm, *refs):
     parts = refs[: 2 * units]
-    out_ref, raw, weight, grad, sems = refs[-5:]
-    s, j = pl.program_id(0), pl.program_id(1)
+    out_hbm, raw, weight, cot, pre, out, grad, part_sem, cot_sem, pre_sem, out_sem = refs[-11:]
     rows = parts[0].shape[0]
     wide = 2 * rows
-    tile = cot_ref.shape[0] // 2
-
-    def copy(i):
-        to = pl.ds(pl.multiple_of(slot_ref[i] * rows, rows), rows)
-        return pltpu.make_async_copy(parts[i], raw.at[i // 2, to], sems.at[i])
-
-    @pl.when((s == 0) & (j == 0))
-    def _():
-        for i in range(2 * units):
-            copy(i).start()
-        for i in range(2 * units):
-            copy(i).wait()
-            if i % 2:
-                u = i // 2
-                weight[:, u * wide : (u + 1) * wide, :] = jnp.swapaxes(raw[u], 0, 1)
-
-    @pl.when(j == 0)
-    def _():
+    pairs, pair = cot.shape[:2]
+    tile = pair // 2
+
+    def part_copy(i):
+        to = pl.ds(pl.multiple_of(where_ref[3 * (at + i // 2) + 1 + i % 2] * rows, rows), rows)
+        return pltpu.make_async_copy(parts[i], raw.at[i // 2, to], part_sem.at[i])
+
+    def cot_copy(s):
+        return pltpu.make_async_copy(cot_hbm.at[pl.ds(s * pair, pair)], cot.at[s], cot_sem.at[s])
+
+    def columns(u):
+        return pl.ds(pl.multiple_of(where_ref[3 * (at + u)] * wide, wide), wide)
+
+    def pre_copy(u):
+        return pltpu.make_async_copy(pre_hbm.at[:, :, columns(u)], pre.at[u], pre_sem.at[u])
+
+    def out_copy(u, s):
+        of = pl.ds(s * pair, pair)
+        return pltpu.make_async_copy(out.at[u, of], out_hbm.at[of, :, columns(u)], out_sem.at[u, s])
+
+    for i in range(2 * units):
+        part_copy(i).start()
+    for s in range(pairs):
+        cot_copy(s).start()
+    for u in range(units):
+        pre_copy(u).start()
+    for u in range(units):
+        part_copy(2 * u).wait()
+        part_copy(2 * u + 1).wait()
+        weight[:, u * wide : (u + 1) * wide, :] = jnp.swapaxes(raw[u], 0, 1)
+    for u in range(units):
+        pre_copy(u).wait()
+
+    @pl.loop(0, pairs)
+    def _(s):
+        cot_copy(s).wait()
         first, second = ids_ref[2 * s], ids_ref[2 * s + 1]
 
         def product(e):
-            full = lax.dot_general(
-                cot_ref[...], weight[e], (((1,), (1,)), ((), ())), preferred_element_type=jnp.float32
-            )
-            return [full[:, i * wide : (i + 1) * wide] for i in range(units)]
-
-        @pl.when(first == second)
-        def _():
-            for i, part in enumerate(product(first)):
-                grad[i] = part
+            return lax.dot_general(cot[s], weight[e], (((1,), (1,)), ((), ())), preferred_element_type=jnp.float32)
+
+        grad[...] = product(first)
 
         @pl.when(first != second)
         def _():
-            for n, e in enumerate((first, second)):
-                for i, part in enumerate(product(e)):
-                    grad[i, n * tile : (n + 1) * tile, :] = part[n * tile : (n + 1) * tile]
-
-    for n in range(2):
-        of = pl.ds(n * tile, tile)
-        live, gate, up, sig = gate_terms(pre_ref.at[of], fill_ref[2 * s + n])
-        base = live * grad[j, of, :]
-        both = jnp.stack([base * up * sig * (1.0 + gate * (1.0 - sig)), base * (gate * sig)])
-        out_ref[of, :, :] = jnp.swapaxes(both.astype(out_ref.dtype), 0, 1)
-
-
-def input_grads(ids, fill, cols, slots, cot, pre_act, parts, into=None):
+            grad[tile:, :] = product(second)[tile:]
+
+        for u in range(units):
+            for n in range(2):
+                of = pl.ds(pl.multiple_of(s * pair + n * tile, tile), tile)
+                live, gate, up, sig = gate_terms(pre.at[u, of], fill_ref[2 * s + n])
+                base = live * grad[n * tile : (n + 1) * tile, u * wide : (u + 1) * wide]
+                both = jnp.stack([base * up * sig * (1.0 + gate * (1.0 - sig)), base * (gate * sig)])
+                out[u, of, :, :] = jnp.swapaxes(both.astype(out.dtype), 0, 1)
+            out_copy(u, s).start()
+
+    for u in range(units):
+        for s in range(pairs):
+            out_copy(u, s).wait()
+
+
+def input_grads(ids, fill, where, at, cot, pre_act, parts, into=None):
     tiles = ids.shape[0]
     rows, width = cot.shape
-    pair = 2 * rows // tiles
+    pairs = tiles // 2
     two = pre_act.shape[1]
     own, experts, _ = parts[0].shape
     units = len(parts) // 2
-    columns = pl.BlockSpec((pair, two, 2 * own), lambda t, j, i, f, c, sl: (t, 0, c[j]))
     anywhere = pl.BlockSpec(memory_space=pl.ANY)
     extra = () if into is None else (into,)
     work = rows * own * units
+    dma = pltpu.SemaphoreType.DMA
     return pl.pallas_call(
-        functools.partial(grad_kernel, units),
-        grid_spec=pltpu.PrefetchScalarGridSpec(
-            num_scalar_prefetch=4,
-            grid=(tiles // 2, units),
-            in_specs=[pl.BlockSpec((pair, width), lambda t, *_: (t, 0)), columns]
-            + [anywhere] * (len(parts) + len(extra)),
-            out_specs=columns,
-            scratch_shapes=[
-                pltpu.VMEM((units, 2 * own, experts, width), cot.dtype),
-                pltpu.VMEM((experts, units * 2 * own, width), cot.dtype),
-                pltpu.VMEM((units, pair, 2 * own), jnp.float32),
-                pltpu.SemaphoreType.DMA((len(parts),)),
-            ],
-        ),
+        functools.partial(grad_kernel, at, units),
+        in_specs=[pl.BlockSpec(memory_space=pltpu.SMEM)] * 3 + [anywhere] * (2 + len(parts) + len(extra)),
+        out_specs=anywhere,
+        scratch_shapes=[
+            pltpu.VMEM((units, 2 * own, experts, width), cot.dtype),
+            pltpu.VMEM((experts, units * 2 * own, width), cot.dtype),
+            pltpu.VMEM((pairs, rows // pairs, width), cot.dtype),
+            pltpu.VMEM((units, rows, two, 2 * own), pre_act.dtype),
+            pltpu.VMEM((units, rows, two, 2 * own), pre_act.dtype),
+            pltpu.VMEM((rows // pairs, units * 2 * own), jnp.float32),
+            dma((len(parts),)),
+            dma((pairs,)),
+            dma((units,)),
+            dma((units, pairs)),
+        ],
         out_shape=jax.ShapeDtypeStruct(pre_act.shape, pre_act.dtype),
-        input_output_aliases={} if into is None else {6 + len(parts): 0},
-        compiler_params=params(58),
+        input_output_aliases={} if into is None else {5 + len(parts): 0},
+        compiler_params=params(32),
         cost_estimate=cost(4 * work * width, 2 * (rows * width + 4 * experts * own * units * width + 16 * work)),
         name="input_grads",
-    )(ids, fill, cols, slots, cot, pre_act, *parts, *extra)
+    )(ids, fill, where, cot, pre_act, *parts, *extra)
 
 
 def body(splits, cotangent, pre_act, down_weight, tile_expert, tile_fill):
@@ -324,20 +384,16 @@
         for i, part in enumerate(held):
             mate = masks[1].index(masks[0][i])
             units.append((part, swap(held[mate]), by_core([m[i] for m in masks]), core))
-    cols = jnp.stack([(blk ^ mask) >> 1 for _, _, mask, _ in units]).astype(jnp.int32)
-    slots = jnp.stack([s for _, _, _, at in units for s in (at, 1 - at)]).astype(jnp.int32)
+    where = jnp.stack([i for _, _, mask, slot in units for i in ((blk ^ mask) >> 1, slot, 1 - slot)])
 
     act = activation_t(tile_fill, pre_act)
     act2 = swap(act)
-    ids = jnp.concatenate([tile_expert, swap(tile_expert)])
+    ids2 = swap(tile_expert)
     act_grad = None
     at = 0
     for size in splits:
         parts = [p for unit in units[at : at + size] for p in unit[:2]]
-        act_grad = input_grads(
-            tile_expert, tile_fill, cols[at : at + size], slots[2 * at : 2 * (at + size)],
-            cotangent, pre_act, parts, act_grad,
-        )
+        act_grad = input_grads(tile_expert, tile_fill, where, at, cotangent, pre_act, parts, act_grad)
         at += size
 
     def granules(step):
@@ -358,13 +414,18 @@
 
     firsts, counts = (0, half - 768), (half - 768, 768)
     sends, keeps = [], []
+    sources = (tile_expert, ids2, pos, act, act2, cotangent, cot2)
     for first, count in zip(firsts, counts):
-        send, keep = terms(ids, pos, act, act2, cotangent, cot2, sizes[0], experts, first, count, blks * owned)
+        (send,) = terms(functools.partial(sent_kernel, first, sizes[0]), sources, count, experts)
         for step in range(len(bits) - 1):
             if step < len(upper):
                 recv = across(send, step)
             else:
                 recv = flip(send, "group", groups, zbits[step - len(upper)])
+            if step == 0:
+                kernel = functools.partial(kept_kernel, first, sizes[0], sizes[1])
+                send, keep = terms(kernel, sources, count, experts, (recv,))
+                continue
             last = step == len(bits) - 2
             send, keep = halve(
                 pos, step + 2, keep, recv, sizes[step + 1], jnp.float32 if last else jnp.bfloat16
@@ -385,7 +446,7 @@
     )
     shape = dict(mesh.shape)
     usual = shape["blk"] == 8 and shape["group"] == 4
-    splits = (1, 2, 1) if usual else (1,) * (shape["blk"] // 2)
+    splits = (1, 1, 1, 1) if usual else (1,) * (shape["blk"] // 2)
 
     def run(*args):
         return body(splits, *args)

time: 192 us -> 189 us (0.984)
  Pallas kernels: 82.9 us -> 71.1 us
  local copies, waits for them, and re-layouts: 1.79 us -> 10 us
  waiting for transfers between devices: 79.5 us -> 83 us
  other arithmetic: 3.03 us -> 0 us
    pallas_call x6 -> x9, Pallas kernels: 73.1 us -> 64.3 us  [the longest x4 37.4 us: input_grads(): pl.pallas_call(functools.partial(grad_kernel, at, units), in_specs=[pl.Bl...]
    unnamed x10 -> x22, local copies, waits for them, and re-layouts: 1.17 us -> 9.88 us
    ppermute x5, waiting for transfers between devices: 55.6 us -> 64.1 us  [across(): lax.ppermute(value, 'blk', [(i, i ^ orders[i & 1][step]) for i in range(b...]
    ppermute x14, starting transfers between devices: 9.85 us -> 14.6 us  [flip(): return lax.ppermute(value, axis, [(i, i ^ mask) for i in range(size)])]
    ppermute x14, waiting for transfers between devices: 21.6 us -> 17 us  [flip(): return lax.ppermute(value, axis, [(i, i ^ mask) for i in range(size)])]
    ppermute x5, starting transfers between devices: 10.3 us -> 6.41 us  [across(): lax.ppermute(value, 'blk', [(i, i ^ orders[i & 1][step]) for i in range(b...]
    pallas_call x8 -> x6, Pallas kernels: 8.65 us -> 5.69 us  [halve(): pl.pallas_call(functools.partial(step_kernel, granules, step), in_specs=[...]
    another operation x4 -> x0, other arithmetic: 2.45 us -> none  [the longest x3 1.89 us: body(): jnp.stack([s for _, _, _, at in units for s in (at, 1 - at)])]
  transfers between devices with their start and end apart: 20 -> 20, of which waited for: 8 -> 7; matrix products, arithmetic and copies ran while one was open for 2% -> 0% of each run, Pallas kernels for 43% -> 37%
where the time goes in v2:
time: 189 us
  waiting for transfers between devices  83 us (44%)
  Pallas kernels  71.1 us (38%)
  starting transfers between devices  24 us (13%)
  local copies, waits for them, and re-layouts  10 us (5%)
    ppermute x5, waiting for transfers between devices, across(): lax.ppermute(value, 'blk', [(i, i ^ orders[i & 1][step]) for i in range(b...  64.1 us
    pallas_call x4, Pallas kernels, input_grads(): pl.pallas_call(functools.partial(grad_kernel, at, units), in_specs=[pl.Bl...  37.4 us
    pallas_call x4, Pallas kernels, terms(): pl.pallas_call(kernel, grid_spec=pltpu.PrefetchScalarGridSpec(num_scalar_...  23.9 us
    ppermute x14, waiting for transfers between devices, flip(): return lax.ppermute(value, axis, [(i, i ^ mask) for i in range(size)])  17 us
    ppermute x14, starting transfers between devices, flip(): return lax.ppermute(value, axis, [(i, i ^ mask) for i in range(size)])  14.6 us
    unnamed x22, local copies, waits for them, and re-layouts  9.88 us
    ppermute x5, starting transfers between devices, across(): lax.ppermute(value, 'blk', [(i, i ^ orders[i & 1][step]) for i in range(b...  6.41 us
    pallas_call x6, Pallas kernels, halve(): pl.pallas_call(functools.partial(step_kernel, granules, step), in_specs=[...  5.69 us
  transfers between devices with their start and end apart: 20, of which 7 were waited for; matrix products, arithmetic and copies ran while one was open for 0% of the time, Pallas kernels for 37%

profile of v2, /device:TPU:0, one launch (start us, length us, event | category | flops | bytes accessed | tf_op | source)
XLA Modules:
  0.0 189.0 jit_solution(1907594999824846005)
XLA Ops:
  1.2 1.9 copy-done.2
  3.7 3.0 %activation_t.1.own_ref = bf16[1024,768]{1,0:T(8,128)(2,1)S(1)} custom-call(s32[6]{0:T(128)S(1)} %copy-done.9, bf16[768,2,1024]{2,1,0:T(2,128)(2,1)S(1)} %copy-done.2), custom_call_target="tpu_custom_call" | custom-call | bytes 4718592 | tf_op jit(solution)/shard_map/activation_t/pallas_call | solution.py:53
  6.9 3.0 %collective-permute-start = (bf16[128,2,3584]{2,1,0:T(2,128)(2,1)}, bf16[128,2,3584]{2,1,0:T(2,128)(2,1)}, u32[]{:S(2)}, u32[]{:S(2)}) collective-permute-start(bf16[128,2,3584]{2,1,0:T(2,128)(2,1)} %refs_0_.1), channel_id=1, source_target_pairs={{2,0},{5,1},{0,2},{7,3},{6,4},{1,5},{4,6},{3,7},{11,8},{12,9},{9,1... | collective-permute-start | bytes 5505032 | tf_op jit(solution)/shard_map/ppermute | solution.py:363
  9.9 2.4 %collective-permute-done.7.ids2_ref = s32[6]{0:T(128)S(1)} collective-permute-done((s32[6]{0:T(128)S(1)}, s32[6]{0:T(128)S(1)}, u32[]{:S(2)}, u32[]{:S(2)}) %collective-permute-start.7) | collective-permute-done | bytes 56 | tf_op jit(solution)/shard_map/ppermute | solution.py:20
  12.3 2.6 %copy-done = bf16[768,3584]{1,0:T(8,128)(2,1)S(1)} copy-done((bf16[768,3584]{1,0:T(8,128)(2,1)S(1)}, bf16[768,3584]{1,0:T(8,128)(2,1)}, u32[]{:S(2)}) %copy-start) | copy-done | bytes 5505048
  14.9 6.4 %terms.4 = bf16[2,512,1024]{2,1,0:T(8,128)(2,1)S(1)} custom-call(s32[6]{0:T(128)S(1)} %copy-done.8, s32[6]{0:T(128)S(1)} %collective-permute-done.7.ids2_ref, s32[6]{0:T(128)S(1)} %stack.84.pos_ref, bf16[1024,768]{1,0:T(8,128)(2,1)S(1)} %activation_t.1.own_ref, bf16[1024,768]{1,0:T(8,128)(2,1)S(1)} %collective-permute-done.8.other_ref, ...), custom_call_target="tpu_custom_call" | custom-call | flops 3221225472 | bytes 12582912 | tf_op jit(solution)/shard_map/terms/pallas_call | solution.py:151
  21.3 2.9 %collective-permute-start.10 = (bf16[2,512,1024]{2,1,0:T(8,128)(2,1)S(1)}, bf16[2,512,1024]{2,1,0:T(8,128)(2,1)S(1)}, u32[]{:S(2)}, u32[]{:S(2)}) collective-permute-start(bf16[2,512,1024]{2,1,0:T(8,128)(2,1)S(1)} %terms.4), channel_id=1, source_target_pairs={{0,2},{1,5},{2,0},{3,7},{4,6},{5,1},{6,4},{7,3},{8,10},{9,13},{10,... | collective-permute-start | bytes 6291464 | tf_op jit(solution)/shard_map/ppermute | solution.py:350
  24.2 5.3 %terms.6 = bf16[2,512,768]{2,1,0:T(8,128)(2,1)S(1)} custom-call(s32[6]{0:T(128)S(1)} %copy-done.8, s32[6]{0:T(128)S(1)} %collective-permute-done.7.ids2_ref, s32[6]{0:T(128)S(1)} %stack.84.pos_ref, bf16[1024,768]{1,0:T(8,128)(2,1)S(1)} %activation_t.1.own_ref, bf16[1024,768]{1,0:T(8,128)(2,1)S(1)} %collective-permute-done.8.other_ref, ...), custom_call_target="tpu_custom_call" | custom-call | flops 2415919104 | bytes 9437184 | tf_op jit(solution)/shard_map/terms/pallas_call | solution.py:151
  29.6 1.8 collective-permute-done.refs_0_
  31.4 6.8 %collective-permute-start.4 = (bf16[128,2,3584]{2,1,0:T(2,128)(2,1)}, bf16[128,2,3584]{2,1,0:T(2,128)(2,1)}, u32[]{:S(2)}, u32[]{:S(2)}) collective-permute-start(bf16[128,2,3584]{2,1,0:T(2,128)(2,1)} %collective-permute-done.refs_0_), channel_id=1, source_target_pairs={{0,8},{8,0},{16,24},{24,16},{1,9},{9,1},{17,25},{25,17},{2,10},{10... | collective-permute-start | bytes 5505032 | tf_op jit(solution)/shard_map/ppermute | solution.py:20
  38.2 1.2 collective-permute-start.1
  39.4 50.9 %collective-permute-done.14.recv = bf16[2,512,768]{2,1,0:T(8,128)(2,1)S(1)} collective-permute-done((bf16[2,512,768]{2,1,0:T(8,128)(2,1)S(1)}, bf16[2,512,768]{2,1,0:T(8,128)(2,1)S(1)}, u32[]{:S(2)}, u32[]{:S(2)}) %collective-permute-start.14) | collective-permute-done | bytes 1572896 | tf_op jit(solution)/shard_map/ppermute | solution.py:350
  90.2 5.5 %terms.7 = (bf16[2,256,768]{2,1,0:T(8,128)(2,1)S(1)}, f32[2,256,768]{2,1,0:T(8,128)S(1)}) custom-call(s32[6]{0:T(128)S(1)} %copy-done.8, s32[6]{0:T(128)S(1)} %collective-permute-done.7.ids2_ref, s32[6]{0:T(128)S(1)} %stack.84.pos_ref, bf16[1024,768]{1,0:T(8,128)(2,1)S(1)} %activation_t.1.own_ref, bf16[1024,768]{1,0:T(8,128)(2,1)S(1)} %collective-permute-done.8.other_ref, ...), custom_call_target="tpu_custom_call" | custom-call | flops 2415919104 | bytes 9437184 | tf_op jit(solution)/shard_map/terms/pallas_call | solution.py:151
  95.8 2.1 %collective-permute-start.15 = (bf16[2,256,768]{2,1,0:T(8,128)(2,1)S(1)}, bf16[2,256,768]{2,1,0:T(8,128)(2,1)S(1)}, u32[]{:S(2)}, u32[]{:S(2)}) collective-permute-start(bf16[2,256,768]{2,1,0:T(8,128)(2,1)S(1)} %get-tuple-element.26), channel_id=1, source_target_pairs={{0,4},{1,3},{2,6},{3,1},{4,0},{5,7},{6,2},{7,5},{8,12},{9,11},{10,... | collective-permute-start | bytes 2359304 | tf_op jit(solution)/shard_map/ppermute | solution.py:350
  97.9 6.7 %terms.5 = (bf16[2,256,1024]{2,1,0:T(8,128)(2,1)S(1)}, f32[2,256,1024]{2,1,0:T(8,128)S(1)}) custom-call(s32[6]{0:T(128)S(1)} %copy-done.8, s32[6]{0:T(128)S(1)} %collective-permute-done.7.ids2_ref, s32[6]{0:T(128)S(1)} %stack.84.pos_ref, bf16[1024,768]{1,0:T(8,128)(2,1)S(1)} %activation_t.1.own_ref, bf16[1024,768]{1,0:T(8,128)(2,1)S(1)} %collective-permute-done.8.other_ref, ...), custom_call_target="tpu_custom_call" | custom-call | flops 3221225472 | bytes 12582912 | tf_op jit(solution)/shard_map/terms/pallas_call | solution.py:151
  105.3 2.6 %collective-permute-done.15.recv_ref = bf16[2,256,768]{2,1,0:T(8,128)(2,1)S(1)} collective-permute-done((bf16[2,256,768]{2,1,0:T(8,128)(2,1)S(1)}, bf16[2,256,768]{2,1,0:T(8,128)(2,1)S(1)}, u32[]{:S(2)}, u32[]{:S(2)}) %collective-permute-start.15) | collective-permute-done | bytes 786464 | tf_op jit(solution)/shard_map/ppermute | solution.py:350
  108.7 10.7 %collective-permute-done.11.recv_ref = bf16[2,256,1024]{2,1,0:T(8,128)(2,1)S(1)} collective-permute-done((bf16[2,256,1024]{2,1,0:T(8,128)(2,1)S(1)}, bf16[2,256,1024]{2,1,0:T(8,128)(2,1)S(1)}, u32[]{:S(2)}, u32[]{:S(2)}) %collective-permute-start.11) | collective-permute-done | bytes 1048608 | tf_op jit(solution)/shard_map/ppermute | solution.py:350
  119.4 1.2 collective-permute-start.16
  120.6 1.7 halve.6
  122.3 1.0 copy-done.4
  123.3 5.8 %collective-permute-done.16.recv_ref = bf16[2,128,768]{2,1,0:T(8,128)(2,1)S(1)} collective-permute-done((bf16[2,128,768]{2,1,0:T(8,128)(2,1)S(1)}, bf16[2,128,768]{2,1,0:T(8,128)(2,1)S(1)}, u32[]{:S(2)}, u32[]{:S(2)}) %collective-permute-start.16) | collective-permute-done | bytes 393248 | tf_op jit(solution)/shard_map/ppermute | solution.py:20
  129.1 1.7 collective-permute-start.12
  131.0 1.2 copy-done.7
  132.9 8.8 %collective-permute-done.12.recv_ref = bf16[2,128,1024]{2,1,0:T(8,128)(2,1)} collective-permute-done((bf16[2,128,1024]{2,1,0:T(8,128)(2,1)}, bf16[2,128,1024]{2,1,0:T(8,128)(2,1)}, u32[]{:S(2)}, u32[]{:S(2)}) %collective-permute-start.12) | collective-permute-done | bytes 524320 | tf_op jit(solution)/shard_map/ppermute | solution.py:20
  141.7 2.6 %collective-permute-start.17 = (bf16[2,64,768]{2,1,0:T(8,128)(2,1)S(1)}, bf16[2,64,768]{2,1,0:T(8,128)(2,1)S(1)}, u32[]{:S(2)}, u32[]{:S(2)}) collective-permute-start(bf16[2,64,768]{2,1,0:T(8,128)(2,1)S(1)} %get-tuple-element.30), channel_id=1, source_target_pairs={{0,16},{8,24},{16,0},{24,8},{1,17},{9,25},{17,1},{25,9},{2,18},{10... | collective-permute-start | bytes 589832 | tf_op jit(solution)/shard_map/ppermute | solution.py:20
  144.3 1.2 halve.7
  145.9 2.6 %copy-done.1 = bf16[768,3584]{1,0:T(8,128)(2,1)S(1)} copy-done((bf16[768,3584]{1,0:T(8,128)(2,1)S(1)}, bf16[768,3584]{1,0:T(8,128)(2,1)}, u32[]{:S(2)}) %copy-start.1) | copy-done | bytes 5505048
  148.5 9.5 %input_grads.4.refs_2_ = bf16[768,2,1024]{2,1,0:T(2,128)(2,1)} custom-call(s32[6]{0:T(128)S(1)} %copy-done.8, s32[6]{0:T(128)S(1)} %copy-done.10, s32[12]{0:T(128)S(1)} %stack.73.where_ref, bf16[768,3584]{1,0:T(8,128)(2,1)S(1)} %copy-done.1, bf16[768,2,1024]{2,1,0:T(2,128)(2,1)S(1)} %copy-done.3, bf16[128,2,3584]{2,1,0:T(2,128)(2,1)} %refs_0_.1, ...), custom_call_target="tpu_custom_call" | custom-call | flops 1409286144 | bytes 15990784 | tf_op jit(solution)/shard_map/input_grads/pallas_call | solution.py:310
  158.0 9.3 %input_grads.5.refs_2_ = bf16[768,2,1024]{2,1,0:T(2,128)(2,1)} custom-call(s32[6]{0:T(128)S(1)} %copy-done.8, s32[6]{0:T(128)S(1)} %copy-done.10, s32[12]{0:T(128)S(1)} %stack.73.where_ref, bf16[768,3584]{1,0:T(8,128)(2,1)S(1)} %copy-done.1, bf16[768,2,1024]{2,1,0:T(2,128)(2,1)S(1)} %copy-done.3, ...), custom_call_target="tpu_custom_call", output_to_operand_aliasing={{}: (7, {})} | custom-call | flops 1409286144 | bytes 15990784 | tf_op jit(solution)/shard_map/input_grads/pallas_call | solution.py:310
  169.2 9.4 %input_grads.6.refs_2_ = bf16[768,2,1024]{2,1,0:T(2,128)(2,1)} custom-call(s32[6]{0:T(128)S(1)} %copy-done.8, s32[6]{0:T(128)S(1)} %copy-done.10, s32[12]{0:T(128)S(1)} %stack.73.where_ref, bf16[768,3584]{1,0:T(8,128)(2,1)S(1)} %copy-done.1, bf16[768,2,1024]{2,1,0:T(2,128)(2,1)S(1)} %copy-done.3, ...), custom_call_target="tpu_custom_call", output_to_operand_aliasing={{}: (7, {})} | custom-call | flops 1409286144 | bytes 15990784 | tf_op jit(solution)/shard_map/input_grads/pallas_call | solution.py:310
  178.6 9.2 %input_grads.7 = bf16[768,2,1024]{2,1,0:T(2,128)(2,1)} custom-call(s32[6]{0:T(128)S(1)} %copy-done.8, s32[6]{0:T(128)S(1)} %copy-done.10, s32[12]{0:T(128)S(1)} %stack.73.where_ref, bf16[768,3584]{1,0:T(8,128)(2,1)S(1)} %copy-done.1, bf16[768,2,1024]{2,1,0:T(2,128)(2,1)S(1)} %copy-done.3, ...), custom_call_target="tpu_custom_call", output_to_operand_aliasing={{}: (7, {})} | custom-call | flops 1409286144 | bytes 15990784 | tf_op jit(solution)/shard_map/input_grads/pallas_call | solution.py:310
  187.9 1.1 finish.1
  (48 shorter events, 6.1 us)
Async XLA Ops:
  0.6 11.7 %collective-permute-start.9 = (bf16[768,3584]{1,0:T(8,128)(2,1)}, bf16[768,3584]{1,0:T(8,128)(2,1)}, u32[]{:S(2)}, u32[]{:S(2)}) collective-permute-start(bf16[768,3584]{1,0:T(8,128)(2,1)} %cot_ref.7), channel_id=1, source_target_pairs={{0,1},{1,0},{2,3},{3,2},{4,5},{5,4},{6,7},{7,6},{8,9},{9,8},{10,11... | collective-permute-start | bytes 16515080 | tf_op jit(solution)/shard_map/ppermute | solution.py:20
  1.2 1.9 copy-start.2
  3.1 0.7 copy-start.9
  3.7 6.1 %copy-start.8 = (s32[6]{0:T(128)S(1)}, s32[6]{0:T(128)}, u32[]{:S(2)}) copy-start(s32[6]{0:T(128)} %ids_ref.15) | copy-start | bytes 76
  6.8 5.5 %collective-permute-start.8 = (bf16[1024,768]{1,0:T(8,128)(2,1)S(1)}, bf16[1024,768]{1,0:T(8,128)(2,1)S(1)}, u32[]{:S(2)}, u32[]{:S(2)}) collective-permute-start(bf16[1024,768]{1,0:T(8,128)(2,1)S(1)} %activation_t.1.own_ref), channel_id=1, source_target_pairs={{0,1},{1,0},{2,3},{3,2},{4,5},{5,4},{6,7},{7,6},{8,9},{9,8},{10,11... | collective-permute-start | bytes 4718600 | tf_op jit(solution)/shard_map/ppermute | solution.py:20
  6.9 24.5 %collective-permute-start = (bf16[128,2,3584]{2,1,0:T(2,128)(2,1)}, bf16[128,2,3584]{2,1,0:T(2,128)(2,1)}, u32[]{:S(2)}, u32[]{:S(2)}) collective-permute-start(bf16[128,2,3584]{2,1,0:T(2,128)(2,1)} %refs_0_.1), channel_id=1, source_target_pairs={{2,0},{5,1},{0,2},{7,3},{6,4},{1,5},{4,6},{3,7},{11,8},{12,9},{9,1... | collective-permute-start | bytes 5505032 | tf_op jit(solution)/shard_map/ppermute | solution.py:363
  9.8 2.5 %collective-permute-start.7 = (s32[6]{0:T(128)S(1)}, s32[6]{0:T(128)S(1)}, u32[]{:S(2)}, u32[]{:S(2)}) collective-permute-start(s32[6]{0:T(128)S(1)} %copy-done.8), channel_id=1, source_target_pairs={{0,1},{1,0},{2,3},{3,2},{4,5},{5,4},{6,7},{7,6},{8,9},{9,8},{10,11... | collective-permute-start | bytes 80 | tf_op jit(solution)/shard_map/ppermute | solution.py:20
  12.3 2.6 %copy-start = (bf16[768,3584]{1,0:T(8,128)(2,1)S(1)}, bf16[768,3584]{1,0:T(8,128)(2,1)}, u32[]{:S(2)}) copy-start(bf16[768,3584]{1,0:T(8,128)(2,1)} %cot_ref.7) | copy-start | bytes 16515076
  21.3 76.6 %collective-permute-start.10 = (bf16[2,512,1024]{2,1,0:T(8,128)(2,1)S(1)}, bf16[2,512,1024]{2,1,0:T(8,128)(2,1)S(1)}, u32[]{:S(2)}, u32[]{:S(2)}) collective-permute-start(bf16[2,512,1024]{2,1,0:T(8,128)(2,1)S(1)} %terms.4), channel_id=1, source_target_pairs={{0,2},{1,5},{2,0},{3,7},{4,6},{5,1},{6,4},{7,3},{8,10},{9,13},{10,... | collective-permute-start | bytes 6291464 | tf_op jit(solution)/shard_map/ppermute | solution.py:350
  29.5 60.7 %collective-permute-start.14 = (bf16[2,512,768]{2,1,0:T(8,128)(2,1)S(1)}, bf16[2,512,768]{2,1,0:T(8,128)(2,1)S(1)}, u32[]{:S(2)}, u32[]{:S(2)}) collective-permute-start(bf16[2,512,768]{2,1,0:T(8,128)(2,1)S(1)} %terms.6), channel_id=1, source_target_pairs={{0,2},{1,5},{2,0},{3,7},{4,6},{5,1},{6,4},{7,3},{8,10},{9,13},{10,... | collective-permute-start | bytes 4718600 | tf_op jit(solution)/shard_map/ppermute | solution.py:350
  31.4 73.4 %collective-permute-start.4 = (bf16[128,2,3584]{2,1,0:T(2,128)(2,1)}, bf16[128,2,3584]{2,1,0:T(2,128)(2,1)}, u32[]{:S(2)}, u32[]{:S(2)}) collective-permute-start(bf16[128,2,3584]{2,1,0:T(2,128)(2,1)} %collective-permute-done.refs_0_), channel_id=1, source_target_pairs={{0,8},{8,0},{16,24},{24,16},{1,9},{9,1},{17,25},{25,17},{2,10},{10... | collective-permute-start | bytes 5505032 | tf_op jit(solution)/shard_map/ppermute | solution.py:20
  38.2 67.0 %collective-permute-start.1 = (bf16[128,2,3584]{2,1,0:T(2,128)(2,1)}, bf16[128,2,3584]{2,1,0:T(2,128)(2,1)}, u32[]{:S(2)}, u32[]{:S(2)}) collective-permute-start(bf16[128,2,3584]{2,1,0:T(2,128)(2,1)} %collective-permute-done.refs_0_), channel_id=1, source_target_pairs={{0,4},{1,3},{2,6},{3,1},{4,0},{5,7},{6,2},{7,5},{8,12},{9,11},{10,... | collective-permute-start | bytes 5505032 | tf_op jit(solution)/shard_map/ppermute | solution.py:350
  95.8 12.1 %collective-permute-start.15 = (bf16[2,256,768]{2,1,0:T(8,128)(2,1)S(1)}, bf16[2,256,768]{2,1,0:T(8,128)(2,1)S(1)}, u32[]{:S(2)}, u32[]{:S(2)}) collective-permute-start(bf16[2,256,768]{2,1,0:T(8,128)(2,1)S(1)} %get-tuple-element.26), channel_id=1, source_target_pairs={{0,4},{1,3},{2,6},{3,1},{4,0},{5,7},{6,2},{7,5},{8,12},{9,11},{10,... | collective-permute-start | bytes 2359304 | tf_op jit(solution)/shard_map/ppermute | solution.py:350
  104.5 14.9 %collective-permute-start.11 = (bf16[2,256,1024]{2,1,0:T(8,128)(2,1)S(1)}, bf16[2,256,1024]{2,1,0:T(8,128)(2,1)S(1)}, u32[]{:S(2)}, u32[]{:S(2)}) collective-permute-start(bf16[2,256,1024]{2,1,0:T(8,128)(2,1)S(1)} %get-tuple-element.19), channel_id=1, source_target_pairs={{0,4},{1,3},{2,6},{3,1},{4,0},{5,7},{6,2},{7,5},{8,12},{9,11},{10,... | collective-permute-start | bytes 3145736 | tf_op jit(solution)/shard_map/ppermute | solution.py:350
  104.6 40.9 %collective-permute-start.6 = (bf16[128,2,3584]{2,1,0:T(2,128)(2,1)}, bf16[128,2,3584]{2,1,0:T(2,128)(2,1)}, u32[]{:S(2)}, u32[]{:S(2)}) collective-permute-start(bf16[128,2,3584]{2,1,0:T(2,128)(2,1)} %refs_0_.1), channel_id=1, source_target_pairs={{0,1},{1,0},{2,3},{3,2},{4,5},{5,4},{6,7},{7,6},{8,9},{9,8},{10,11... | collective-permute-start | bytes 5505032 | tf_op jit(solution)/shard_map/ppermute | solution.py:20
  104.7 64.5 %collective-permute-start.3 = (bf16[128,2,3584]{2,1,0:T(2,128)(2,1)}, bf16[128,2,3584]{2,1,0:T(2,128)(2,1)}, u32[]{:S(2)}, u32[]{:S(2)}) collective-permute-start(bf16[128,2,3584]{2,1,0:T(2,128)(2,1)} %collective-permute-done.refs_0_), channel_id=1, source_target_pairs={{0,1},{1,0},{2,3},{3,2},{4,5},{5,4},{6,7},{7,6},{8,9},{9,8},{10,11... | collective-permute-start | bytes 5505032 | tf_op jit(solution)/shard_map/ppermute | solution.py:20
  105.2 64.0 %collective-permute-start.5 = (bf16[128,2,3584]{2,1,0:T(2,128)(2,1)}, bf16[128,2,3584]{2,1,0:T(2,128)(2,1)}, u32[]{:S(2)}, u32[]{:S(2)}) collective-permute-start(bf16[128,2,3584]{2,1,0:T(2,128)(2,1)} %collective-permute-done.4.refs_1_), channel_id=1, source_target_pairs={{0,1},{1,0},{2,3},{3,2},{4,5},{5,4},{6,7},{7,6},{8,9},{9,8},{10,11... | collective-permute-start | bytes 5505032 | tf_op jit(solution)/shard_map/ppermute | solution.py:20
  107.9 70.7 %collective-permute-start.2 = (bf16[128,2,3584]{2,1,0:T(2,128)(2,1)}, bf16[128,2,3584]{2,1,0:T(2,128)(2,1)}, u32[]{:S(2)}, u32[]{:S(2)}) collective-permute-start(bf16[128,2,3584]{2,1,0:T(2,128)(2,1)} %collective-permute-done.1.refs_0_), channel_id=1, source_target_pairs={{0,1},{1,0},{2,3},{3,2},{4,5},{5,4},{6,7},{7,6},{8,9},{9,8},{10,11... | collective-permute-start | bytes 5505032 | tf_op jit(solution)/shard_map/ppermute | solution.py:20
  108.7 13.6 %copy-start.6 = (f32[2,128,768]{2,1,0:T(8,128)}, f32[2,128,768]{2,1,0:T(8,128)S(1)}, u32[]{:S(2)}) copy-start(f32[2,128,768]{2,1,0:T(8,128)S(1)} %get-tuple-element.27.keep_ref) | copy-start | bytes 2359300
  119.4 9.7 %collective-permute-start.16 = (bf16[2,128,768]{2,1,0:T(8,128)(2,1)S(1)}, bf16[2,128,768]{2,1,0:T(8,128)(2,1)S(1)}, u32[]{:S(2)}, u32[]{:S(2)}) collective-permute-start(bf16[2,128,768]{2,1,0:T(8,128)(2,1)S(1)} %get-tuple-element.28), channel_id=1, source_target_pairs={{0,8},{8,0},{16,24},{24,16},{1,9},{9,1},{17,25},{25,17},{2,10},{10... | collective-permute-start | bytes 1179656 | tf_op jit(solution)/shard_map/ppermute | solution.py:20
  120.6 25.3 %copy-start.3 = (bf16[768,2,1024]{2,1,0:T(2,128)(2,1)S(1)}, bf16[768,2,1024]{2,1,0:T(2,128)(2,1)}, u32[]{:S(2)}) copy-start(bf16[768,2,1024]{2,1,0:T(2,128)(2,1)} %pre_ref.1) | copy-start | bytes 9437188
  122.3 1.0 copy-start.4
  123.3 22.6 %copy-start.10 = (s32[6]{0:T(128)S(1)}, s32[6]{0:T(128)}, u32[]{:S(2)}) copy-start(s32[6]{0:T(128)} %fill_ref.9) | copy-start | bytes 76
  129.1 12.5 %collective-permute-start.12 = (bf16[2,128,1024]{2,1,0:T(8,128)(2,1)}, bf16[2,128,1024]{2,1,0:T(8,128)(2,1)}, u32[]{:S(2)}, u32[]{:S(2)}) collective-permute-start(bf16[2,128,1024]{2,1,0:T(8,128)(2,1)} %get-tuple-element.21), channel_id=1, source_target_pairs={{0,8},{8,0},{16,24},{24,16},{1,9},{9,1},{17,25},{25,17},{2,10},{10... | collective-permute-start | bytes 1572872 | tf_op jit(solution)/shard_map/ppermute | solution.py:20
  131.0 13.3 %copy-start.5 = (f32[2,128,1024]{2,1,0:T(8,128)S(1)}, f32[2,128,1024]{2,1,0:T(8,128)}, u32[]{:S(2)}) copy-start(f32[2,128,1024]{2,1,0:T(8,128)} %copy-done.4) | copy-start | bytes 3145732
  131.0 1.2 copy-start.7
  141.7 25.6 %collective-permute-start.17 = (bf16[2,64,768]{2,1,0:T(8,128)(2,1)S(1)}, bf16[2,64,768]{2,1,0:T(8,128)(2,1)S(1)}, u32[]{:S(2)}, u32[]{:S(2)}) collective-permute-start(bf16[2,64,768]{2,1,0:T(8,128)(2,1)S(1)} %get-tuple-element.30), channel_id=1, source_target_pairs={{0,16},{8,24},{16,0},{24,8},{1,17},{9,25},{17,1},{25,9},{2,18},{10... | collective-permute-start | bytes 589832 | tf_op jit(solution)/shard_map/ppermute | solution.py:20
  145.5 22.5 %collective-permute-start.13 = (bf16[2,64,1024]{2,1,0:T(8,128)(2,1)S(1)}, bf16[2,64,1024]{2,1,0:T(8,128)(2,1)S(1)}, u32[]{:S(2)}, u32[]{:S(2)}) collective-permute-start(bf16[2,64,1024]{2,1,0:T(8,128)(2,1)S(1)} %get-tuple-element.23), channel_id=1, source_target_pairs={{0,16},{8,24},{16,0},{24,8},{1,17},{9,25},{17,1},{25,9},{2,18},{10... | collective-permute-start | bytes 786440 | tf_op jit(solution)/shard_map/ppermute | solution.py:20
  145.9 2.6 %copy-start.1 = (bf16[768,3584]{1,0:T(8,128)(2,1)S(1)}, bf16[768,3584]{1,0:T(8,128)(2,1)}, u32[]{:S(2)}) copy-start(bf16[768,3584]{1,0:T(8,128)(2,1)} %cot_ref.7) | copy-start | bytes 16515076
  167.9 19.9 %collective-permute-start.19 = (f32[2,32,768]{2,1,0:T(8,128)S(1)}, f32[2,32,768]{2,1,0:T(8,128)S(1)}, u32[]{:S(2)}, u32[]{:S(2)}) collective-permute-start(f32[2,32,768]{2,1,0:T(8,128)S(1)} %get-tuple-element.33), channel_id=1, source_target_pairs={{0,1},{1,0},{2,3},{3,2},{4,5},{5,4},{6,7},{7,6},{8,9},{9,8},{10,11... | collective-permute-start | bytes 589832 | tf_op jit(solution)/shard_map/ppermute | solution.py:20
  168.7 19.2 %collective-permute-start.18 = (f32[2,32,1024]{2,1,0:T(8,128)S(1)}, f32[2,32,1024]{2,1,0:T(8,128)S(1)}, u32[]{:S(2)}, u32[]{:S(2)}) collective-permute-start(f32[2,32,1024]{2,1,0:T(8,128)S(1)} %get-tuple-element.32), channel_id=1, source_target_pairs={{0,1},{1,0},{2,3},{3,2},{4,5},{5,4},{6,7},{7,6},{8,9},{9,8},{10,11... | collective-permute-start | bytes 786440 | tf_op jit(solution)/shard_map/ppermute | solution.py:20

commit v3 on v2

--- a/solution.py
+++ b/solution.py
@@ -59,7 +59,7 @@
             out_specs=pl.BlockSpec((hidden, block), lambda t, f: (0, t)),
         ),
         out_shape=jax.ShapeDtypeStruct((hidden, rows), pre_act.dtype),
-        compiler_params=params(32),
+        compiler_params=params(18),
         cost_estimate=cost(0, 6 * rows * hidden),
         name="activation_t",
     )(tile_fill, pre_act)
@@ -165,7 +165,7 @@
             ],
         ),
         out_shape=[jax.ShapeDtypeStruct((experts, hidden // part, count), kind) for part, kind in kinds],
-        compiler_params=params(32),
+        compiler_params=params(18 if recv else 58),
         cost_estimate=cost(2 * hidden * 2 * rows * count, 6 * hidden * count + 8 * rows * count),
         name="terms",
     )(*sources, *recv)
@@ -230,21 +230,18 @@
     )(core, *keeps, *others)
 
 
-def grad_kernel(at, units, ids_ref, fill_ref, where_ref, cot_hbm, pre_hbm, *refs):
+def grad_kernel(at, units, ids_ref, fill_ref, where_ref, cot, pre_hbm, *refs):
     parts = refs[: 2 * units]
-    out_hbm, raw, weight, cot, pre, out, grad, part_sem, cot_sem, pre_sem, out_sem = refs[-11:]
+    out_hbm, raw, weight, pre, out, grad, part_sem, pre_sem, out_sem = refs[-9:]
     rows = parts[0].shape[0]
     wide = 2 * rows
-    pairs, pair = cot.shape[:2]
-    tile = pair // 2
+    tile = cot.shape[0] // ids_ref.shape[0]
+    pair, pairs = 2 * tile, ids_ref.shape[0] // 2
 
     def part_copy(i):
         to = pl.ds(pl.multiple_of(where_ref[3 * (at + i // 2) + 1 + i % 2] * rows, rows), rows)
         return pltpu.make_async_copy(parts[i], raw.at[i // 2, to], part_sem.at[i])
 
-    def cot_copy(s):
-        return pltpu.make_async_copy(cot_hbm.at[pl.ds(s * pair, pair)], cot.at[s], cot_sem.at[s])
-
     def columns(u):
         return pl.ds(pl.multiple_of(where_ref[3 * (at + u)] * wide, wide), wide)
 
@@ -257,8 +254,6 @@
 
     for i in range(2 * units):
         part_copy(i).start()
-    for s in range(pairs):
-        cot_copy(s).start()
     for u in range(units):
         pre_copy(u).start()
     for u in range(units):
@@ -270,11 +265,11 @@
 
     @pl.loop(0, pairs)
     def _(s):
-        cot_copy(s).wait()
         first, second = ids_ref[2 * s], ids_ref[2 * s + 1]
 
         def product(e):
-            return lax.dot_general(cot[s], weight[e], (((1,), (1,)), ((), ())), preferred_element_type=jnp.float32)
+            rows_of = cot[pl.ds(pl.multiple_of(s * pair, pair), pair), :]
+            return lax.dot_general(rows_of, weight[e], (((1,), (1,)), ((), ())), preferred_element_type=jnp.float32)
 
         grad[...] = product(first)
 
@@ -309,23 +304,23 @@
     dma = pltpu.SemaphoreType.DMA
     return pl.pallas_call(
         functools.partial(grad_kernel, at, units),
-        in_specs=[pl.BlockSpec(memory_space=pltpu.SMEM)] * 3 + [anywhere] * (2 + len(parts) + len(extra)),
+        in_specs=[pl.BlockSpec(memory_space=pltpu.SMEM)] * 3
+        + [pl.BlockSpec(memory_space=pltpu.VMEM)]
+        + [anywhere] * (1 + len(parts) + len(extra)),
         out_specs=anywhere,
         scratch_shapes=[
             pltpu.VMEM((units, 2 * own, experts, width), cot.dtype),
             pltpu.VMEM((experts, units * 2 * own, width), cot.dtype),
-            pltpu.VMEM((pairs, rows // pairs, width), cot.dtype),
             pltpu.VMEM((units, rows, two, 2 * own), pre_act.dtype),
             pltpu.VMEM((units, rows, two, 2 * own), pre_act.dtype),
             pltpu.VMEM((rows // pairs, units * 2 * own), jnp.float32),
             dma((len(parts),)),
-            dma((pairs,)),
             dma((units,)),
             dma((units, pairs)),
         ],
         out_shape=jax.ShapeDtypeStruct(pre_act.shape, pre_act.dtype),
         input_output_aliases={} if into is None else {5 + len(parts): 0},
-        compiler_params=params(32),
+        compiler_params=params(18),
         cost_estimate=cost(4 * work * width, 2 * (rows * width + 4 * experts * own * units * width + 16 * work)),
         name="input_grads",
     )(ids, fill, where, cot, pre_act, *parts, *extra)

time: 189 us -> 191 us (1.011)
  Pallas kernels: 71.1 us -> 78.2 us
  waiting for transfers between devices: 83 us -> 79.3 us
    pallas_call x4, Pallas kernels: 23.9 us -> 30.5 us  [terms(): pl.pallas_call(kernel, grid_spec=pltpu.PrefetchScalarGridSpec(num_scalar_...]
    unnamed x22 -> x32, local copies, waits for them, and re-layouts: 9.88 us -> 7.84 us
  transfers between devices with their start and end apart: 20 -> 20, of which waited for: 7 -> 7; matrix products, arithmetic and copies ran while one was open for 0% -> 0% of each run, Pallas kernels for 37% -> 40%
where the time goes in v3:
time: 191 us
  waiting for transfers between devices  79.3 us (42%)
  Pallas kernels  78.2 us (41%)
  starting transfers between devices  24 us (13%)
  local copies, waits for them, and re-layouts  8.61 us (5%)
    ppermute x5, waiting for transfers between devices, across(): lax.ppermute(value, 'blk', [(i, i ^ orders[i & 1][step]) for i in range(b...  63.9 us
    pallas_call x4, Pallas kernels, input_grads(): pl.pallas_call(functools.partial(grad_kernel, at, units), in_specs=[pl.Bl...  37 us
    pallas_call x4, Pallas kernels, terms(): pl.pallas_call(kernel, grid_spec=pltpu.PrefetchScalarGridSpec(num_scalar_...  30.5 us
    ppermute x14, waiting for transfers between devices, flip(): return lax.ppermute(value, axis, [(i, i ^ mask) for i in range(size)])  15.2 us
    ppermute x14, starting transfers between devices, flip(): return lax.ppermute(value, axis, [(i, i ^ mask) for i in range(size)])  14.6 us
    unnamed x32, local copies, waits for them, and re-layouts  7.84 us
    ppermute x5, starting transfers between devices, across(): lax.ppermute(value, 'blk', [(i, i ^ orders[i & 1][step]) for i in range(b...  6.45 us
    pallas_call x6, Pallas kernels, halve(): pl.pallas_call(functools.partial(step_kernel, granules, step), in_specs=[...  5.72 us
  transfers between devices with their start and end apart: 20, of which 7 were waited for; matrix products, arithmetic and copies ran while one was open for 0% of the time, Pallas kernels for 40%

profile of v3, /device:TPU:0, one launch (start us, length us, event | category | flops | bytes accessed | tf_op | source)
XLA Modules:
  0.0 191.1 jit_solution(13910196472392052171)
XLA Ops:
  1.2 1.9 copy-done.1
  3.7 3.8 %activation_t.1.own_ref = bf16[1024,768]{1,0:T(8,128)(2,1)} custom-call(s32[6]{0:T(128)S(1)} %copy-done.10, bf16[768,2,1024]{2,1,0:T(2,128)(2,1)S(1)} %copy-done.1), custom_call_target="tpu_custom_call" | custom-call | bytes 4718592 | tf_op jit(solution)/shard_map/activation_t/pallas_call | solution.py:53
  7.6 3.0 %collective-permute-start = (bf16[128,2,3584]{2,1,0:T(2,128)(2,1)}, bf16[128,2,3584]{2,1,0:T(2,128)(2,1)}, u32[]{:S(2)}, u32[]{:S(2)}) collective-permute-start(bf16[128,2,3584]{2,1,0:T(2,128)(2,1)} %refs_0_.1), channel_id=1, source_target_pairs={{2,0},{5,1},{0,2},{7,3},{6,4},{1,5},{4,6},{3,7},{11,8},{12,9},{9,1... | collective-permute-start | bytes 5505032 | tf_op jit(solution)/shard_map/ppermute | solution.py:358
  10.6 0.7 stack.84.pos_ref
  11.3 1.2 collective-permute-done.7.ids2_ref
  12.9 8.5 %terms.4 = bf16[2,512,1024]{2,1,0:T(8,128)(2,1)} custom-call(s32[6]{0:T(128)} %ids_ref.15, s32[6]{0:T(128)} %copy-done.12, s32[6]{0:T(128)} %stack.84.pos_ref, bf16[1024,768]{1,0:T(8,128)(2,1)} %activation_t.1.own_ref, bf16[1024,768]{1,0:T(8,128)(2,1)} %collective-permute-done.8.other_ref, bf16[768,3584]{1,0:T(8,128)(2,1)} %cot_ref.7, ...), custom_call_target="tpu_custom_call" | custom-call | flops 3221225472 | bytes 12582912 | tf_op jit(solution)/shard_map/terms/pallas_call | solution.py:151
  21.5 2.9 %collective-permute-start.10 = (bf16[2,512,1024]{2,1,0:T(8,128)(2,1)}, bf16[2,512,1024]{2,1,0:T(8,128)(2,1)}, u32[]{:S(2)}, u32[]{:S(2)}) collective-permute-start(bf16[2,512,1024]{2,1,0:T(8,128)(2,1)} %terms.4), channel_id=1, source_target_pairs={{0,2},{1,5},{2,0},{3,7},{4,6},{5,1},{6,4},{7,3},{8,10},{9,13},{10,... | collective-permute-start | bytes 6291464 | tf_op jit(solution)/shard_map/ppermute | solution.py:345
  24.4 7.4 %terms.6 = bf16[2,512,768]{2,1,0:T(8,128)(2,1)} custom-call(s32[6]{0:T(128)} %ids_ref.15, s32[6]{0:T(128)} %copy-done.12, s32[6]{0:T(128)} %stack.84.pos_ref, bf16[1024,768]{1,0:T(8,128)(2,1)} %activation_t.1.own_ref, bf16[1024,768]{1,0:T(8,128)(2,1)} %collective-permute-done.8.other_ref, bf16[768,3584]{1,0:T(8,128)(2,1)} %cot_ref.7, ...), custom_call_target="tpu_custom_call" | custom-call | flops 2415919104 | bytes 9437184 | tf_op jit(solution)/shard_map/terms/pallas_call | solution.py:151
  32.1 7.1 %collective-permute-start.4 = (bf16[128,2,3584]{2,1,0:T(2,128)(2,1)}, bf16[128,2,3584]{2,1,0:T(2,128)(2,1)}, u32[]{:S(2)}, u32[]{:S(2)}) collective-permute-start(bf16[128,2,3584]{2,1,0:T(2,128)(2,1)} %collective-permute-done.refs_0_), channel_id=1, source_target_pairs={{0,8},{8,0},{16,24},{24,16},{1,9},{9,1},{17,25},{25,17},{2,10},{10... | collective-permute-start | bytes 5505032 | tf_op jit(solution)/shard_map/ppermute | solution.py:20
  39.1 1.2 collective-permute-start.1
  40.4 50.6 %collective-permute-done.14.recv = bf16[2,512,768]{2,1,0:T(8,128)(2,1)S(1)} collective-permute-done((bf16[2,512,768]{2,1,0:T(8,128)(2,1)}, bf16[2,512,768]{2,1,0:T(8,128)(2,1)S(1)}, u32[]{:S(2)}, u32[]{:S(2)}) %collective-permute-start.14) | collective-permute-done | bytes 1572896 | tf_op jit(solution)/shard_map/ppermute | solution.py:345
  91.0 6.2 %terms.7 = (bf16[2,256,768]{2,1,0:T(8,128)(2,1)S(1)}, f32[2,256,768]{2,1,0:T(8,128)S(1)}) custom-call(s32[6]{0:T(128)S(1)} %copy-done.9, s32[6]{0:T(128)S(1)} %copy-done.13, s32[6]{0:T(128)S(1)} %copy-done.7, bf16[1024,768]{1,0:T(8,128)(2,1)} %activation_t.1.own_ref, bf16[1024,768]{1,0:T(8,128)(2,1)} %collective-permute-done.8.other_ref, ...), custom_call_target="tpu_custom_call" | custom-call | flops 2415919104 | bytes 9437184 | tf_op jit(solution)/shard_map/terms/pallas_call | solution.py:151
  97.2 2.1 %collective-permute-start.15 = (bf16[2,256,768]{2,1,0:T(8,128)(2,1)S(1)}, bf16[2,256,768]{2,1,0:T(8,128)(2,1)S(1)}, u32[]{:S(2)}, u32[]{:S(2)}) collective-permute-start(bf16[2,256,768]{2,1,0:T(8,128)(2,1)S(1)} %get-tuple-element.26), channel_id=1, source_target_pairs={{0,4},{1,3},{2,6},{3,1},{4,0},{5,7},{6,2},{7,5},{8,12},{9,11},{10,... | collective-permute-start | bytes 2359304 | tf_op jit(solution)/shard_map/ppermute | solution.py:345
  99.3 8.5 %terms.5 = (bf16[2,256,1024]{2,1,0:T(8,128)(2,1)S(1)}, f32[2,256,1024]{2,1,0:T(8,128)S(1)}) custom-call(s32[6]{0:T(128)S(1)} %copy-done.9, s32[6]{0:T(128)S(1)} %copy-done.13, s32[6]{0:T(128)S(1)} %copy-done.7, bf16[1024,768]{1,0:T(8,128)(2,1)} %activation_t.1.own_ref, bf16[1024,768]{1,0:T(8,128)(2,1)} %collective-permute-done.8.other_ref, ...), custom_call_target="tpu_custom_call" | custom-call | flops 3221225472 | bytes 12582912 | tf_op jit(solution)/shard_map/terms/pallas_call | solution.py:151
  108.5 0.8 collective-permute-done.15.recv_ref
  109.3 0.8 halve.9
  110.1 12.5 %collective-permute-done.11.recv_ref = bf16[2,256,1024]{2,1,0:T(8,128)(2,1)S(1)} collective-permute-done((bf16[2,256,1024]{2,1,0:T(8,128)(2,1)S(1)}, bf16[2,256,1024]{2,1,0:T(8,128)(2,1)S(1)}, u32[]{:S(2)}, u32[]{:S(2)}) %collective-permute-start.11) | collective-permute-done | bytes 1048608 | tf_op jit(solution)/shard_map/ppermute | solution.py:345
  122.7 1.0 collective-permute-start.16
  123.7 1.8 halve.6
  125.4 1.0 copy-done.3
  126.4 5.5 %collective-permute-done.16.recv_ref = bf16[2,128,768]{2,1,0:T(8,128)(2,1)S(1)} collective-permute-done((bf16[2,128,768]{2,1,0:T(8,128)(2,1)S(1)}, bf16[2,128,768]{2,1,0:T(8,128)(2,1)S(1)}, u32[]{:S(2)}, u32[]{:S(2)}) %collective-permute-start.16) | collective-permute-done | bytes 393248 | tf_op jit(solution)/shard_map/ppermute | solution.py:20
  131.9 1.7 collective-permute-start.12
  133.7 1.2 copy-done.6
  135.6 8.5 %collective-permute-done.12.recv_ref = bf16[2,128,1024]{2,1,0:T(8,128)(2,1)} collective-permute-done((bf16[2,128,1024]{2,1,0:T(8,128)(2,1)}, bf16[2,128,1024]{2,1,0:T(8,128)(2,1)}, u32[]{:S(2)}, u32[]{:S(2)}) %collective-permute-start.12) | collective-permute-done | bytes 524320 | tf_op jit(solution)/shard_map/ppermute | solution.py:20
  144.1 2.6 %collective-permute-start.17 = (bf16[2,64,768]{2,1,0:T(8,128)(2,1)S(1)}, bf16[2,64,768]{2,1,0:T(8,128)(2,1)S(1)}, u32[]{:S(2)}, u32[]{:S(2)}) collective-permute-start(bf16[2,64,768]{2,1,0:T(8,128)(2,1)S(1)} %get-tuple-element.30), channel_id=1, source_target_pairs={{0,16},{8,24},{16,0},{24,8},{1,17},{9,25},{17,1},{25,9},{2,18},{10... | collective-permute-start | bytes 589832 | tf_op jit(solution)/shard_map/ppermute | solution.py:20
  146.7 1.2 halve.7
  148.4 2.6 %copy-done = bf16[768,3584]{1,0:T(8,128)(2,1)S(1)} copy-done((bf16[768,3584]{1,0:T(8,128)(2,1)S(1)}, bf16[768,3584]{1,0:T(8,128)(2,1)}, u32[]{:S(2)}) %copy-start) | copy-done | bytes 5505048
  150.9 9.2 %input_grads.4.refs_2_ = bf16[768,2,1024]{2,1,0:T(2,128)(2,1)} custom-call(s32[6]{0:T(128)S(1)} %copy-done.9, s32[6]{0:T(128)S(1)} %copy-done.11, s32[12]{0:T(128)S(1)} %stack.73.where_ref, bf16[768,3584]{1,0:T(8,128)(2,1)S(1)} %copy-done, bf16[768,2,1024]{2,1,0:T(2,128)(2,1)S(1)} %copy-done.2, bf16[128,2,3584]{2,1,0:T(2,128)(2,1)} %refs_0_.1, ...), custom_call_target="tpu_custom_call" | custom-call | flops 1409286144 | bytes 15990784 | tf_op jit(solution)/shard_map/input_grads/pallas_call | solution.py:305
  160.2 9.2 %input_grads.5.refs_2_ = bf16[768,2,1024]{2,1,0:T(2,128)(2,1)} custom-call(s32[6]{0:T(128)S(1)} %copy-done.9, s32[6]{0:T(128)S(1)} %copy-done.11, s32[12]{0:T(128)S(1)} %stack.73.where_ref, bf16[768,3584]{1,0:T(8,128)(2,1)S(1)} %copy-done, bf16[768,2,1024]{2,1,0:T(2,128)(2,1)S(1)} %copy-done.2, ...), custom_call_target="tpu_custom_call", output_to_operand_aliasing={{}: (7, {})} | custom-call | flops 1409286144 | bytes 15990784 | tf_op jit(solution)/shard_map/input_grads/pallas_call | solution.py:305
  171.3 9.3 %input_grads.6.refs_2_ = bf16[768,2,1024]{2,1,0:T(2,128)(2,1)} custom-call(s32[6]{0:T(128)S(1)} %copy-done.9, s32[6]{0:T(128)S(1)} %copy-done.11, s32[12]{0:T(128)S(1)} %stack.73.where_ref, bf16[768,3584]{1,0:T(8,128)(2,1)S(1)} %copy-done, bf16[768,2,1024]{2,1,0:T(2,128)(2,1)S(1)} %copy-done.2, ...), custom_call_target="tpu_custom_call", output_to_operand_aliasing={{}: (7, {})} | custom-call | flops 1409286144 | bytes 15990784 | tf_op jit(solution)/shard_map/input_grads/pallas_call | solution.py:305
  180.7 9.2 %input_grads.7 = bf16[768,2,1024]{2,1,0:T(2,128)(2,1)} custom-call(s32[6]{0:T(128)S(1)} %copy-done.9, s32[6]{0:T(128)S(1)} %copy-done.11, s32[12]{0:T(128)S(1)} %stack.73.where_ref, bf16[768,3584]{1,0:T(8,128)(2,1)S(1)} %copy-done, bf16[768,2,1024]{2,1,0:T(2,128)(2,1)S(1)} %copy-done.2, ...), custom_call_target="tpu_custom_call", output_to_operand_aliasing={{}: (7, {})} | custom-call | flops 1409286144 | bytes 15990784 | tf_op jit(solution)/shard_map/input_grads/pallas_call | solution.py:305
  189.9 1.1 finish.1
  (59 shorter events, 5.9 us)
Async XLA Ops:
  0.6 11.8 %collective-permute-start.9 = (bf16[768,3584]{1,0:T(8,128)(2,1)}, bf16[768,3584]{1,0:T(8,128)(2,1)}, u32[]{:S(2)}, u32[]{:S(2)}) collective-permute-start(bf16[768,3584]{1,0:T(8,128)(2,1)} %cot_ref.7), channel_id=1, source_target_pairs={{0,1},{1,0},{2,3},{3,2},{4,5},{5,4},{6,7},{7,6},{8,9},{9,8},{10,11... | collective-permute-start | bytes 16515080 | tf_op jit(solution)/shard_map/ppermute | solution.py:20
  1.2 1.9 copy-start.1
  3.7 6.8 %copy-start.8 = (s32[6]{0:T(128)S(1)}, s32[6]{0:T(128)}, u32[]{:S(2)}) copy-start(s32[6]{0:T(128)} %ids_ref.15) | copy-start | bytes 76
  3.7 87.2 %slice-start = ((s8[5505024]{0:T(1024)(128)(4,1)}), s8[1310720]{0:T(1024)(128)(4,1)S(1)}, s32[]{:S(2)}) async-start(s8[5505024]{0:T(1024)(128)(4,1)} %bitcast.13), calls=%async_computation | async-start | bytes 2621440
  7.6 4.9 %collective-permute-start.8 = (bf16[1024,768]{1,0:T(8,128)(2,1)}, bf16[1024,768]{1,0:T(8,128)(2,1)}, u32[]{:S(2)}, u32[]{:S(2)}) collective-permute-start(bf16[1024,768]{1,0:T(8,128)(2,1)} %activation_t.1.own_ref), channel_id=1, source_target_pairs={{0,1},{1,0},{2,3},{3,2},{4,5},{5,4},{6,7},{7,6},{8,9},{9,8},{10,11... | collective-permute-start | bytes 4718600 | tf_op jit(solution)/shard_map/ppermute | solution.py:20
  7.6 24.5 %collective-permute-start = (bf16[128,2,3584]{2,1,0:T(2,128)(2,1)}, bf16[128,2,3584]{2,1,0:T(2,128)(2,1)}, u32[]{:S(2)}, u32[]{:S(2)}) collective-permute-start(bf16[128,2,3584]{2,1,0:T(2,128)(2,1)} %refs_0_.1), channel_id=1, source_target_pairs={{2,0},{5,1},{0,2},{7,3},{6,4},{1,5},{4,6},{3,7},{11,8},{12,9},{9,1... | collective-permute-start | bytes 5505032 | tf_op jit(solution)/shard_map/ppermute | solution.py:358
  10.6 1.9 collective-permute-start.7
  11.3 79.7 %slice-start.1 = ((s8[5505024]{0:T(1024)(128)(4,1)}), s8[4194304]{0:T(1024)(128)(4,1)S(1)}, s32[]{:S(2)}) async-start(s8[5505024]{0:T(1024)(128)(4,1)} %bitcast.13), calls=%async_computation.1 | async-start | bytes 8388608
  21.5 69.5 %copy-start.7 = (s32[6]{0:T(128)S(1)}, s32[6]{0:T(128)}, u32[]{:S(2)}) copy-start(s32[6]{0:T(128)} %stack.84.pos_ref) | copy-start | bytes 76
  21.5 69.5 %copy-start.9 = (s32[6]{0:T(128)S(1)}, s32[6]{0:T(128)}, u32[]{:S(2)}) copy-start(s32[6]{0:T(128)} %ids_ref.15) | copy-start | bytes 76
  21.5 69.5 %copy-start.13 = (s32[6]{0:T(128)S(1)}, s32[6]{0:T(128)}, u32[]{:S(2)}) copy-start(s32[6]{0:T(128)} %copy-done.12) | copy-start | bytes 76
  21.5 77.8 %collective-permute-start.10 = (bf16[2,512,1024]{2,1,0:T(8,128)(2,1)}, bf16[2,512,1024]{2,1,0:T(8,128)(2,1)}, u32[]{:S(2)}, u32[]{:S(2)}) collective-permute-start(bf16[2,512,1024]{2,1,0:T(8,128)(2,1)} %terms.4), channel_id=1, source_target_pairs={{0,2},{1,5},{2,0},{3,7},{4,6},{5,1},{6,4},{7,3},{8,10},{9,13},{10,... | collective-permute-start | bytes 6291464 | tf_op jit(solution)/shard_map/ppermute | solution.py:345
  31.8 59.2 %collective-permute-start.14 = (bf16[2,512,768]{2,1,0:T(8,128)(2,1)}, bf16[2,512,768]{2,1,0:T(8,128)(2,1)S(1)}, u32[]{:S(2)}, u32[]{:S(2)}) collective-permute-start(bf16[2,512,768]{2,1,0:T(8,128)(2,1)} %terms.6), channel_id=1, source_target_pairs={{0,2},{1,5},{2,0},{3,7},{4,6},{5,1},{6,4},{7,3},{8,10},{9,13},{10,... | collective-permute-start | bytes 4718600 | tf_op jit(solution)/shard_map/ppermute | solution.py:345
  32.1 75.9 %collective-permute-start.4 = (bf16[128,2,3584]{2,1,0:T(2,128)(2,1)}, bf16[128,2,3584]{2,1,0:T(2,128)(2,1)}, u32[]{:S(2)}, u32[]{:S(2)}) collective-permute-start(bf16[128,2,3584]{2,1,0:T(2,128)(2,1)} %collective-permute-done.refs_0_), channel_id=1, source_target_pairs={{0,8},{8,0},{16,24},{24,16},{1,9},{9,1},{17,25},{25,17},{2,10},{10... | collective-permute-start | bytes 5505032 | tf_op jit(solution)/shard_map/ppermute | solution.py:20
  39.1 69.3 %collective-permute-start.1 = (bf16[128,2,3584]{2,1,0:T(2,128)(2,1)}, bf16[128,2,3584]{2,1,0:T(2,128)(2,1)}, u32[]{:S(2)}, u32[]{:S(2)}) collective-permute-start(bf16[128,2,3584]{2,1,0:T(2,128)(2,1)} %collective-permute-done.refs_0_), channel_id=1, source_target_pairs={{0,4},{1,3},{2,6},{3,1},{4,0},{5,7},{6,2},{7,5},{8,12},{9,11},{10,... | collective-permute-start | bytes 5505032 | tf_op jit(solution)/shard_map/ppermute | solution.py:345
  97.2 12.1 %collective-permute-start.15 = (bf16[2,256,768]{2,1,0:T(8,128)(2,1)S(1)}, bf16[2,256,768]{2,1,0:T(8,128)(2,1)S(1)}, u32[]{:S(2)}, u32[]{:S(2)}) collective-permute-start(bf16[2,256,768]{2,1,0:T(8,128)(2,1)S(1)} %get-tuple-element.26), channel_id=1, source_target_pairs={{0,4},{1,3},{2,6},{3,1},{4,0},{5,7},{6,2},{7,5},{8,12},{9,11},{10,... | collective-permute-start | bytes 2359304 | tf_op jit(solution)/shard_map/ppermute | solution.py:345
  107.8 14.9 %collective-permute-start.11 = (bf16[2,256,1024]{2,1,0:T(8,128)(2,1)S(1)}, bf16[2,256,1024]{2,1,0:T(8,128)(2,1)S(1)}, u32[]{:S(2)}, u32[]{:S(2)}) collective-permute-start(bf16[2,256,1024]{2,1,0:T(8,128)(2,1)S(1)} %get-tuple-element.19), channel_id=1, source_target_pairs={{0,4},{1,3},{2,6},{3,1},{4,0},{5,7},{6,2},{7,5},{8,12},{9,11},{10,... | collective-permute-start | bytes 3145736 | tf_op jit(solution)/shard_map/ppermute | solution.py:345
  107.9 40.1 %collective-permute-start.6 = (bf16[128,2,3584]{2,1,0:T(2,128)(2,1)}, bf16[128,2,3584]{2,1,0:T(2,128)(2,1)}, u32[]{:S(2)}, u32[]{:S(2)}) collective-permute-start(bf16[128,2,3584]{2,1,0:T(2,128)(2,1)} %refs_0_.1), channel_id=1, source_target_pairs={{0,1},{1,0},{2,3},{3,2},{4,5},{5,4},{6,7},{7,6},{8,9},{9,8},{10,11... | collective-permute-start | bytes 5505032 | tf_op jit(solution)/shard_map/ppermute | solution.py:20
  108.0 63.3 %collective-permute-start.3 = (bf16[128,2,3584]{2,1,0:T(2,128)(2,1)}, bf16[128,2,3584]{2,1,0:T(2,128)(2,1)}, u32[]{:S(2)}, u32[]{:S(2)}) collective-permute-start(bf16[128,2,3584]{2,1,0:T(2,128)(2,1)} %collective-permute-done.refs_0_), channel_id=1, source_target_pairs={{0,1},{1,0},{2,3},{3,2},{4,5},{5,4},{6,7},{7,6},{8,9},{9,8},{10,11... | collective-permute-start | bytes 5505032 | tf_op jit(solution)/shard_map/ppermute | solution.py:20
  108.5 62.9 %collective-permute-start.5 = (bf16[128,2,3584]{2,1,0:T(2,128)(2,1)}, bf16[128,2,3584]{2,1,0:T(2,128)(2,1)}, u32[]{:S(2)}, u32[]{:S(2)}) collective-permute-start(bf16[128,2,3584]{2,1,0:T(2,128)(2,1)} %collective-permute-done.4.refs_1_), channel_id=1, source_target_pairs={{0,1},{1,0},{2,3},{3,2},{4,5},{5,4},{6,7},{7,6},{8,9},{9,8},{10,11... | collective-permute-start | bytes 5505032 | tf_op jit(solution)/shard_map/ppermute | solution.py:20
  109.3 71.4 %collective-permute-start.2 = (bf16[128,2,3584]{2,1,0:T(2,128)(2,1)}, bf16[128,2,3584]{2,1,0:T(2,128)(2,1)}, u32[]{:S(2)}, u32[]{:S(2)}) collective-permute-start(bf16[128,2,3584]{2,1,0:T(2,128)(2,1)} %collective-permute-done.1.refs_0_), channel_id=1, source_target_pairs={{0,1},{1,0},{2,3},{3,2},{4,5},{5,4},{6,7},{7,6},{8,9},{9,8},{10,11... | collective-permute-start | bytes 5505032 | tf_op jit(solution)/shard_map/ppermute | solution.py:20
  110.1 15.3 %copy-start.5 = (f32[2,128,768]{2,1,0:T(8,128)}, f32[2,128,768]{2,1,0:T(8,128)S(1)}, u32[]{:S(2)}) copy-start(f32[2,128,768]{2,1,0:T(8,128)S(1)} %get-tuple-element.27.keep_ref) | copy-start | bytes 2359300
  122.7 9.2 %collective-permute-start.16 = (bf16[2,128,768]{2,1,0:T(8,128)(2,1)S(1)}, bf16[2,128,768]{2,1,0:T(8,128)(2,1)S(1)}, u32[]{:S(2)}, u32[]{:S(2)}) collective-permute-start(bf16[2,128,768]{2,1,0:T(8,128)(2,1)S(1)} %get-tuple-element.28), channel_id=1, source_target_pairs={{0,8},{8,0},{16,24},{24,16},{1,9},{9,1},{17,25},{25,17},{2,10},{10... | collective-permute-start | bytes 1179656 | tf_op jit(solution)/shard_map/ppermute | solution.py:20
  123.7 24.7 %copy-start.2 = (bf16[768,2,1024]{2,1,0:T(2,128)(2,1)S(1)}, bf16[768,2,1024]{2,1,0:T(2,128)(2,1)}, u32[]{:S(2)}) copy-start(bf16[768,2,1024]{2,1,0:T(2,128)(2,1)} %pre_ref.1) | copy-start | bytes 9437188
  126.4 22.0 %copy-start.11 = (s32[6]{0:T(128)S(1)}, s32[6]{0:T(128)}, u32[]{:S(2)}) copy-start(s32[6]{0:T(128)} %fill_ref.9) | copy-start | bytes 76
  131.9 12.2 %collective-permute-start.12 = (bf16[2,128,1024]{2,1,0:T(8,128)(2,1)}, bf16[2,128,1024]{2,1,0:T(8,128)(2,1)}, u32[]{:S(2)}, u32[]{:S(2)}) collective-permute-start(bf16[2,128,1024]{2,1,0:T(8,128)(2,1)} %get-tuple-element.21), channel_id=1, source_target_pairs={{0,8},{8,0},{16,24},{24,16},{1,9},{9,1},{17,25},{25,17},{2,10},{10... | collective-permute-start | bytes 1572872 | tf_op jit(solution)/shard_map/ppermute | solution.py:20
  133.7 13.0 %copy-start.4 = (f32[2,128,1024]{2,1,0:T(8,128)S(1)}, f32[2,128,1024]{2,1,0:T(8,128)}, u32[]{:S(2)}) copy-start(f32[2,128,1024]{2,1,0:T(8,128)} %copy-done.3) | copy-start | bytes 3145732
  144.1 25.3 %collective-permute-start.17 = (bf16[2,64,768]{2,1,0:T(8,128)(2,1)S(1)}, bf16[2,64,768]{2,1,0:T(8,128)(2,1)S(1)}, u32[]{:S(2)}, u32[]{:S(2)}) collective-permute-start(bf16[2,64,768]{2,1,0:T(8,128)(2,1)S(1)} %get-tuple-element.30), channel_id=1, source_target_pairs={{0,16},{8,24},{16,0},{24,8},{1,17},{9,25},{17,1},{25,9},{2,18},{10... | collective-permute-start | bytes 589832 | tf_op jit(solution)/shard_map/ppermute | solution.py:20
  147.9 22.2 %collective-permute-start.13 = (bf16[2,64,1024]{2,1,0:T(8,128)(2,1)S(1)}, bf16[2,64,1024]{2,1,0:T(8,128)(2,1)S(1)}, u32[]{:S(2)}, u32[]{:S(2)}) collective-permute-start(bf16[2,64,1024]{2,1,0:T(8,128)(2,1)S(1)} %get-tuple-element.23), channel_id=1, source_target_pairs={{0,16},{8,24},{16,0},{24,8},{1,17},{9,25},{17,1},{25,9},{2,18},{10... | collective-permute-start | bytes 786440 | tf_op jit(solution)/shard_map/ppermute | solution.py:20
  148.4 2.6 %copy-start = (bf16[768,3584]{1,0:T(8,128)(2,1)S(1)}, bf16[768,3584]{1,0:T(8,128)(2,1)}, u32[]{:S(2)}) copy-start(bf16[768,3584]{1,0:T(8,128)(2,1)} %cot_ref.7) | copy-start | bytes 16515076
  170.0 19.9 %collective-permute-start.19 = (f32[2,32,768]{2,1,0:T(8,128)S(1)}, f32[2,32,768]{2,1,0:T(8,128)S(1)}, u32[]{:S(2)}, u32[]{:S(2)}) collective-permute-start(f32[2,32,768]{2,1,0:T(8,128)S(1)} %get-tuple-element.33), channel_id=1, source_target_pairs={{0,1},{1,0},{2,3},{3,2},{4,5},{5,4},{6,7},{7,6},{8,9},{9,8},{10,11... | collective-permute-start | bytes 589832 | tf_op jit(solution)/shard_map/ppermute | solution.py:20
  170.7 19.2 %collective-permute-start.18 = (f32[2,32,1024]{2,1,0:T(8,128)S(1)}, f32[2,32,1024]{2,1,0:T(8,128)S(1)}, u32[]{:S(2)}, u32[]{:S(2)}) collective-permute-start(f32[2,32,1024]{2,1,0:T(8,128)S(1)} %get-tuple-element.32), channel_id=1, source_target_pairs={{0,1},{1,0},{2,3},{3,2},{4,5},{5,4},{6,7},{7,6},{8,9},{9,8},{10,11... | collective-permute-start | bytes 786440 | tf_op jit(solution)/shard_map/ppermute | solution.py:20
  (4 other events, 3.4 us)
